TPU v7x, 512 devices: a whole 4x8x8 slice. The times are simulated.
512 devices in a mesh: panel: 2 (over x_hi), rad: 8 (over z), ang: 32 (over y, x_lo, core).
Axes of the slice: x: 4 (x_hi: 2, x_lo: 2; x = x_hi * 2 + x_lo), y: 8, z: 8, core: 2. Of those that a mesh axis runs over, the one named last changes fastest.
Arguments:
- adj_final: float32 [2, 7, 8, 256, 1536], P('panel', None, 'rad', 'ang'), may hold values from -6 to 6
- cond: float32 [2, 8, 256, 1536], P('panel', 'rad', 'ang'), may hold values from 0.5 to 1.5
- diffus: float32 [7], replicated, may hold values from 0.02 to 0.1
- couple: float32 [7, 7], replicated, may hold values from -0.1 to 0.1
- ghost_row: int32 [2, 4, 256], replicated, may hold values from 0 to 255
- ghost_col: int32 [2, 4, 256], replicated, may hold values from 0 to 1535
- ghost_wt: float32 [2, 4, 256], replicated, may hold values from 0.5 to 1.5
- obs_dest: int32 [2, 8, 8192, 1], P('panel', 'rad', 'ang'), may hold values from 0 to 31; in each aligned block of 256 rows (0 to 255, 256 to 511, ..., all dimensions but the last counted through in order) at most 16 rows name the same one
- obs_cell: int32 [2, 8, 4, 8192], P('panel', 'rad', None, 'ang'), may hold values from 0 to 12287
- obs_wt: float32 [2, 8, 4, 8192], P('panel', 'rad', None, 'ang'), may hold values from 0.2 to 1
- misfit: float32 [2, 8, 2, 8192], P('panel', 'rad', None, 'ang'), may hold values from -6 to 6
Outputs:
- adj_start: float32 [2, 7, 8, 256, 1536], P('panel', None, 'rad', 'ang')
Inputs may be any that keep to these rules, and one draw needn't show every extreme that they name: `obs_dest`: owner tile, within the observation's own panel, whose outermost layer holds it; among the 256 observations of one device at most 16 name one owner. `obs_cell`: row within the owner's tile times 1536 plus column.
All inputs are finite; a program needn't handle non-finite values.
Results may differ from a plain program's by a relative error of at most 0.000088.
Values sent between devices are 32-bit elements; how exact they have to be, the bound alone decides.
A program may use at most 64 MiB of HBM per device.

v0:
```python
import jax
import jax.numpy as jnp
from jax import lax
from jax.sharding import PartitionSpec as P


def swapped(x, axis, apart):
    return lax.ppermute(x, axis, [(i, i ^ 1 << apart) for i in range(lax.axis_size(axis))])


def extended(block, sides, width):
    for axis, dim in sides:
        count = lax.axis_size(axis)
        forward = [(i, i + 1) for i in range(count - 1)]
        backward = [(target, source) for source, target in forward]
        low = lax.ppermute(
            lax.slice_in_dim(block, block.shape[dim] - width, None, axis=dim), axis, forward
        )
        high = lax.ppermute(lax.slice_in_dim(block, 0, width, axis=dim), axis, backward)
        block = jnp.concatenate([low, block, high], axis=dim)
    return block


def deposit(inbox, cells_total):
    values = inbox[:8].reshape(2, -1)
    cells = inbox[8:].astype(jnp.int32).reshape(-1)
    dense = jnp.zeros((2, cells_total), jnp.float32)
    return dense.at[:, cells].add(values, mode="drop")


def route_obs(obs_dest, obs_cell, obs_wt, misfit, cells_total):
    target = obs_dest[0, 0, :, 0]
    count = target.shape[0]
    owners = lax.axis_size("ang")
    slots = 2 * count // owners
    onehot = (target[:, None] == jnp.arange(owners, dtype=jnp.int32)[None]).astype(jnp.int32)
    before = jnp.cumsum(onehot, axis=0) - onehot
    ranking = jnp.sum(before * onehot, axis=1)
    position = target * slots + ranking
    values = (misfit[0, 0][:, None, :] * obs_wt[0, 0][None]).reshape(8, count)
    payload = jnp.concatenate([values, obs_cell[0, 0].astype(jnp.float32)], axis=0)
    blank = jnp.concatenate(
        [
            jnp.zeros((8, owners * slots), jnp.float32),
            jnp.full((4, owners * slots), cells_total, jnp.float32),
        ],
        axis=0,
    )
    outbox = blank.at[:, position].set(payload)
    inbox = lax.all_to_all(outbox, "ang", split_axis=1, concat_axis=1, tiled=True)
    dense = deposit(inbox, cells_total)
    return lax.psum(dense, "rad")


def other_edges(edges):
    across = swapped(edges, "panel", 0)
    return lax.all_gather(across, "ang", axis=3, tiled=True)


def ghost_terms(scaled_own, row_start, central_rows, ghost_row, ghost_col, ghost_wt):
    fields, layers, tile_rows, columns = scaled_own.shape
    edges = jnp.stack([scaled_own[..., 0], scaled_own[..., -1]], axis=2)
    gathered = other_edges(edges)
    values = gathered[:, :, :, None, :] * ghost_wt[None, None]
    local_row = ghost_row - row_start
    inside = (local_row >= 0) & (local_row < central_rows)
    flat_index = jnp.where(inside, local_row * columns + ghost_col, central_rows * columns).reshape(
        -1
    )
    target = jnp.zeros((fields, layers, central_rows * columns), jnp.float32)
    target = target.at[:, :, flat_index].add(values.reshape(fields, layers, -1), mode="drop")
    return target.reshape(fields, layers, central_rows, columns)


def finish(padded, centre, ghost_add, source, couple, row_start, total_rows):
    middle = padded[:, 1:-1, 1:-1]
    lap = padded[:, 2:, 1:-1] + padded[:, :-2, 1:-1] + padded[:, 1:-1, 2:] + padded[:, 1:-1, :-2]
    west = jnp.pad(middle[..., :-1], ((0, 0), (0, 0), (0, 0), (1, 0)))
    east = jnp.pad(middle[..., 1:], ((0, 0), (0, 0), (0, 0), (0, 1)))
    lap = lap + west + east - 6.0 * middle
    coupled = jnp.einsum("ec,elrk->clrk", couple, centre, precision=lax.Precision.HIGHEST)
    updated = centre + lap + ghost_add + coupled
    updated = updated.at[3].add(source)
    global_rows = row_start + jnp.arange(centre.shape[2], dtype=jnp.int32)
    inside = ((global_rows >= 0) & (global_rows < total_rows)).astype(jnp.float32)
    return updated * inside[None, None, :, None]


def shallow_step(
    adjoint, coeff, source, couple, row_start, total_rows, ghost_row, ghost_col, ghost_wt
):
    scaled = coeff * adjoint
    padded = extended(scaled, (("rad", 1), ("ang", 2)), 1)
    ghost_add = ghost_terms(scaled, row_start, adjoint.shape[2], ghost_row, ghost_col, ghost_wt)
    return finish(padded, adjoint, ghost_add, source, couple, row_start, total_rows)


def body(
    adj_final,
    cond,
    diffus,
    couple,
    ghost_row,
    ghost_col,
    ghost_wt,
    obs_dest,
    obs_cell,
    obs_wt,
    misfit,
):
    adjoint = adj_final[0]
    conduct = cond[0]
    fields, layers, tile_rows, columns = adjoint.shape
    total_rows = tile_rows * lax.axis_size("ang")
    row_start = lax.axis_index("ang") * tile_rows
    outer = (lax.axis_index("rad") == lax.axis_size("rad") - 1).astype(jnp.float32)
    forcing = route_obs(obs_dest, obs_cell, obs_wt, misfit, tile_rows * columns)
    sources = []
    for moment in range(2):
        blank = jnp.zeros((layers, tile_rows, columns), jnp.float32)
        sources.append(
            blank.at[layers - 1].set(forcing[moment].reshape(tile_rows, columns) * outer)
        )
    coeff = diffus[:, None, None, None] * conduct[None]
    first = shallow_step(
        adjoint, coeff, sources[1], couple, row_start, total_rows, ghost_row, ghost_col, ghost_wt
    )
    final = shallow_step(
        first, coeff, sources[0], couple, row_start, total_rows, ghost_row, ghost_col, ghost_wt
    )
    return final[None]


def solution(mesh):
    placed = (
        P("panel", None, "rad", "ang", None),
        P("panel", "rad", "ang", None),
        P(),
        P(),
        P(),
        P(),
        P(),
        P("panel", "rad", "ang", None),
        P("panel", "rad", None, "ang"),
        P("panel", "rad", None, "ang"),
        P("panel", "rad", None, "ang"),
    )
    return jax.shard_map(
        body,
        mesh=mesh,
        in_specs=placed,
        out_specs=P("panel", None, "rad", "ang", None),
        check_vma=False,
    )
```

profile of v0, /device:TPU:1, one launch (start us, length us, event | category | flops | bytes accessed | tf_op | source)
XLA Modules:
  0.0 364.4 jit_solution(14950490070713340924)
XLA Ops:
  6.5 1.2 multiply_multiply_fusion.1
  7.8 1.3 collective-permute-start
  9.1 5.5 %collective-permute-start.1 = (f32[7,1,8,1536]{3,0,2,1:T(8,128)S(1)}, f32[7,1,8,1536]{3,0,2,1:T(8,128)S(1)}, u32[]{:S(2)}, u32[]{:S(2)}) collective-permute-start(f32[7,1,8,1536]{3,0,2,1:T(8,128)S(1)} %multiply_multiply_fusion.1), channel_id=1, source_target_pairs={{0,32},{32,64},{64,96},{96,128},{128,160},{160,192},{192,224},{1,3... | collective-permute-start | bytes 1032200 | tf_op jit(solution)/shard_map/ppermute | solution.py:16
  14.6 0.1 copy.73
  14.8 0.1 copy.74
  14.9 4.7 %collective-permute-start.4 = (f32[7,1,2,8]{3,2,0,1:T(2,128)S(1)}, f32[7,1,2,8]{3,2,0,1:T(2,128)S(1)}, u32[]{:S(2)}, u32[]{:S(2)}) collective-permute-start(f32[7,1,2,8]{3,2,0,1:T(2,128)S(1)} %pad_maximum_fusion.18), channel_id=1, source_target_pairs={{0,256},{256,0},{1,257},{257,1},{2,258},{258,2},{3,259},{259,3},{4... | collective-permute-start | bytes 1352 | tf_op jit(solution)/shard_map/ppermute | solution.py:8
  19.6 0.7 fusion.37
  20.3 0.6 reduce-window.6
  20.8 0.2 slice_reduce_fusion
  21.1 0.8 fusion.36
  21.8 0.7 compare_select_fusion.2
  22.5 0.9 copy.119
  23.5 0.7 broadcast_multiply_fusion
  24.2 0.7 convert_bitcast_fusion
  24.9 0.1 copy.82
  25.0 1.3 scatter_fusion
  26.3 0.3 copy.83
  26.5 0.8 reshape.458
  27.3 8.5 %all-to-all-start = ((f32[32,1,192]{2,1,0:T(1,128)}), f32[32,1,192]{2,1,0:T(1,128)S(1)}, u32[]{:S(2)}, u32[]{:S(2)}) async-start(f32[32,1,192]{2,1,0:T(1,128)} %reshape.458), calls=%async_computation | async-start | bytes 65536 | tf_op jit(solution)/shard_map/all_to_all | solution.py:50
  35.9 0.2 fusion.42
  36.1 0.7 add_select_fusion
  36.9 0.7 copy.108
  37.6 0.1 copy.75
  37.7 35.1 %all_gather.6 = f32[7,1,2,256]{0,2,1,3:T(2,128)S(1)} all-gather(f32[7,1,2,8]{0,2,1,3:T(2,128)S(1)} %copy.75), channel_id=1, replica_groups=mesh['panel'=2,'rad'=8,'ang'=32] {'ang'}, dimensions={3}, use_global_device_ids=true | all-gather | bytes 14784 | tf_op jit(solution)/shard_map/all_gather | solution.py:57
  72.8 15.5 %scatter_custom_fusion = f32[7,12288]{0,1:T(8,128)} fusion(s32[2048]{0:T(1024)S(1)} %bitcast.114, f32[]{:T(128)} %constant.119.clone.1, f32[7,1,2048]{0,2,1:T(8,128)S(1)} %bitcast.92, f32[2048]{0:T(1024)S(1)} %bitcast.104), kind=kCustom, calls=%fused_computation.10 | custom fusion | flops 28672 | bytes 1400836 | tf_op jit(solution)/shard_map/scatter-add | solution.py:71
  88.3 4.4 %copy.78 = f32[7,1,8,1536]{3,0,2,1:T(8,128)S(1)} copy(f32[7,1,8,1536]{0,3,2,1:T(8,128)} %bitcast.90) | data formatting | bytes 688128 | tf_op jit(solution)/shard_map/reshape | solution.py:72
  92.8 0.5 broadcast.324
  93.3 0.7 reduce.14
  94.0 0.1 reshape.459
  94.2 0.1 reshape.428
  94.3 1.4 copy.87
  95.8 0.1 copy.85
  95.9 0.1 convert_element_type.51
  96.0 14.8 %scatter_custom_fusion.2 = f32[2,12288]{0,1:T(8,128)} fusion(s32[2048]{0:T(1024)S(1)} %bitcast.116, f32[2048,2]{1,0:T(8,128)} %copy.87, f32[]{:T(128)} %constant.119.clone.1), kind=kCustom, calls=%fused_computation.12 | custom fusion | flops 4096 | bytes 98816 | tf_op jit(solution)/shard_map/scatter-add | solution.py:28
  110.9 0.7 pad_maximum_fusion.17
  111.6 2.1 collective-permute-start.2
  113.7 3.8 %collective-permute-start.3 = (f32[7,3,1,1536]{3,0,2,1:T(8,128)S(1)}, f32[7,3,1,1536]{3,0,2,1:T(8,128)S(1)}, u32[]{:S(2)}, u32[]{:S(2)}) collective-permute-start(f32[7,3,1,1536]{3,0,2,1:T(8,128)S(1)} %get-tuple-element.58), channel_id=1, source_target_pairs={{0,1},{1,2},{2,3},{3,4},{4,5},{5,6},{6,7},{7,8},{8,9},{9,10},{10,1... | collective-permute-start | bytes 387080 | tf_op jit(solution)/shard_map/ppermute | solution.py:16
  117.5 148.5 %all-reduce.6.cloned.1.call-done = f32[2,12288]{0,1:T(8,128)} async-done(((f32[2,12288]{0,1:T(8,128)}), f32[2,12288]{0,1:T(8,128)}) %all-reduce.6.cloned.1.call-update) | async-done | bytes 98320 | tf_op jit(solution)/shard_map/psum | solution.py:52
  266.0 9.6 %fusion = (f32[12288]{0:T(1024)S(1)}, f32[12288]{0:T(1024)S(1)}) fusion(f32[2,12288]{0,1:T(8,128)} %all-reduce.6.cloned.1.call-done, f32[]{:T(128)S(6)} %convert_element_type.52), kind=kLoop, calls=%fused_computation.5 | loop fusion | flops 24576 | bytes 196612 | tf_op jit(solution)/shard_map/mul | solution.py:122
  275.7 0.7 copy-done.3
  276.4 1.9 fusion.9
  278.2 0.1 slice_add_fusion.1
  278.3 0.6 scatter-add.33
  278.9 0.1 multiply_multiply_fusion
  279.0 1.3 collective-permute-start.5
  280.3 4.0 %collective-permute-start.6 = (f32[7,1,8,1536]{3,0,2,1:T(8,128)S(1)}, f32[7,1,8,1536]{3,0,2,1:T(8,128)S(1)}, u32[]{:S(2)}, u32[]{:S(2)}) collective-permute-start(f32[7,1,8,1536]{3,0,2,1:T(8,128)S(1)} %multiply_multiply_fusion), channel_id=1, source_target_pairs={{0,32},{32,64},{64,96},{96,128},{128,160},{160,192},{192,224},{1,3... | collective-permute-start | bytes 1032200 | tf_op jit(solution)/shard_map/ppermute | solution.py:16
  284.4 0.1 copy.89
  284.5 0.1 copy.90
  284.7 4.6 %collective-permute-start.9 = (f32[7,1,2,8]{3,2,0,1:T(2,128)S(1)}, f32[7,1,2,8]{3,2,0,1:T(2,128)S(1)}, u32[]{:S(2)}, u32[]{:S(2)}) collective-permute-start(f32[7,1,2,8]{3,2,0,1:T(2,128)S(1)} %pad_maximum_fusion.19), channel_id=1, source_target_pairs={{0,256},{256,0},{1,257},{257,1},{2,258},{258,2},{3,259},{259,3},{4... | collective-permute-start | bytes 1352 | tf_op jit(solution)/shard_map/ppermute | solution.py:8
  289.3 1.6 collective-permute-done.5
  290.9 0.9 collective-permute-done.6
  291.8 0.7 pad_maximum_fusion.14
  292.5 3.8 %collective-permute-start.7 = (f32[7,3,1,1536]{3,0,2,1:T(8,128)}, f32[7,3,1,1536]{3,0,2,1:T(8,128)}, u32[]{:S(2)}, u32[]{:S(2)}) collective-permute-start(f32[7,3,1,1536]{3,0,2,1:T(8,128)} %get-tuple-element.55), channel_id=1, source_target_pairs={{1,0},{2,1},{3,2},{4,3},{5,4},{6,5},{7,6},{8,7},{9,8},{10,9},{11,1... | collective-permute-start | bytes 387080 | tf_op jit(solution)/shard_map/ppermute | solution.py:19
  296.3 3.0 collective-permute-start.8
  299.3 0.2 fusion.40
  299.4 0.1 copy.91
  299.5 34.7 %all_gather.7 = f32[7,1,2,256]{0,2,1,3:T(2,128)S(1)} all-gather(f32[7,1,2,8]{0,2,1,3:T(2,128)S(1)} %copy.91), channel_id=1, replica_groups=mesh['panel'=2,'rad'=8,'ang'=32] {'ang'}, dimensions={3}, use_global_device_ids=true | all-gather | bytes 14784 | tf_op jit(solution)/shard_map/all_gather | solution.py:57
  334.3 15.5 %scatter_custom_fusion.3 = f32[7,12288]{0,1:T(8,128)} fusion(s32[2048]{0:T(1024)S(1)} %bitcast.115, f32[]{:T(128)} %constant.119.clone.1, f32[7,1,2048]{0,2,1:T(8,128)S(1)} %bitcast.91, f32[2048]{0:T(1024)S(1)} %bitcast.105), kind=kCustom, calls=%fused_computation.8 | custom fusion | flops 28672 | bytes 1400836 | tf_op jit(solution)/shard_map/scatter-add | solution.py:71
  349.8 4.4 %copy.94 = f32[7,1,8,1536]{3,0,2,1:T(8,128)S(1)} copy(f32[7,1,8,1536]{0,3,2,1:T(8,128)} %bitcast.89) | data formatting | bytes 688128 | tf_op jit(solution)/shard_map/reshape | solution.py:72
  354.3 1.6 fusion.8
  355.9 0.1 slice_add_fusion
  355.9 0.6 scatter-add.35
  356.5 0.1 multiply_bitcast_fusion
  356.6 0.9 copy.97
  (41 shorter events, 0.7 us)
Async XLA Ops:
  6.5 269.8 %copy-start = (f32[7,7]{1,0:T(8,128)S(1)}, f32[7,7]{1,0:T(8,128)}, u32[]{:S(2)}) copy-start(f32[7,7]{1,0:T(8,128)} %param.22) | copy-start | bytes 592
  7.8 103.1 %collective-permute-start = (f32[7,1,8,1536]{3,0,2,1:T(8,128)S(1)}, f32[7,1,8,1536]{3,0,2,1:T(8,128)S(1)}, u32[]{:S(2)}, u32[]{:S(2)}) collective-permute-start(f32[7,1,8,1536]{3,0,2,1:T(8,128)S(1)} %multiply_multiply_fusion.1), channel_id=1, source_target_pairs={{32,0},{64,32},{96,64},{128,96},{160,128},{192,160},{224,192},{33,... | collective-permute-start | bytes 1032200 | tf_op jit(solution)/shard_map/ppermute | solution.py:19
  9.1 101.8 %collective-permute-start.1 = (f32[7,1,8,1536]{3,0,2,1:T(8,128)S(1)}, f32[7,1,8,1536]{3,0,2,1:T(8,128)S(1)}, u32[]{:S(2)}, u32[]{:S(2)}) collective-permute-start(f32[7,1,8,1536]{3,0,2,1:T(8,128)S(1)} %multiply_multiply_fusion.1), channel_id=1, source_target_pairs={{0,32},{32,64},{64,96},{96,128},{128,160},{160,192},{192,224},{1,3... | collective-permute-start | bytes 1032200 | tf_op jit(solution)/shard_map/ppermute | solution.py:16
  14.9 22.7 %collective-permute-start.4 = (f32[7,1,2,8]{3,2,0,1:T(2,128)S(1)}, f32[7,1,2,8]{3,2,0,1:T(2,128)S(1)}, u32[]{:S(2)}, u32[]{:S(2)}) collective-permute-start(f32[7,1,2,8]{3,2,0,1:T(2,128)S(1)} %pad_maximum_fusion.18), channel_id=1, source_target_pairs={{0,256},{256,0},{1,257},{257,1},{2,258},{258,2},{3,259},{259,3},{4... | collective-permute-start | bytes 1352 | tf_op jit(solution)/shard_map/ppermute | solution.py:8
  27.3 65.4 %all-to-all-start = ((f32[32,1,192]{2,1,0:T(1,128)}), f32[32,1,192]{2,1,0:T(1,128)S(1)}, u32[]{:S(2)}, u32[]{:S(2)}) async-start(f32[32,1,192]{2,1,0:T(1,128)} %reshape.458), calls=%async_computation | async-start | bytes 65536 | tf_op jit(solution)/shard_map/all_to_all | solution.py:50
  35.9 230.2 %all-reduce.6.cloned.1.call-start = ((), (), s32[]{:S(2)}) async-start(), calls=%async_computation.1 | async-start | bytes 12582912 | tf_op jit(solution)/shard_map/psum | solution.py:52
  111.6 164.1 %collective-permute-start.2 = (f32[7,3,1,1536]{3,0,2,1:T(8,128)}, f32[7,3,1,1536]{3,0,2,1:T(8,128)S(1)}, u32[]{:S(2)}, u32[]{:S(2)}) collective-permute-start(f32[7,3,1,1536]{3,0,2,1:T(8,128)} %get-tuple-element.57), channel_id=1, source_target_pairs={{1,0},{2,1},{3,2},{4,3},{5,4},{6,5},{7,6},{8,7},{9,8},{10,9},{11,1... | collective-permute-start | bytes 387080 | tf_op jit(solution)/shard_map/ppermute | solution.py:19
  113.7 162.7 %copy-start.1 = (f32[1,7,1,8,1536]{4,3,2,1,0:T(8,128)S(1)}, f32[1,7,1,8,1536]{4,3,2,1,0:T(8,128)}, u32[]{:S(2)}) copy-start(f32[1,7,1,8,1536]{4,3,2,1,0:T(8,128)} %param.19) | copy-start | bytes 1032196
  113.7 165.2 %copy-start.2 = (f32[1,1,8,1536]{3,2,1,0:T(8,128)S(1)}, f32[1,1,8,1536]{3,2,1,0:T(8,128)}, u32[]{:S(2)}) copy-start(f32[1,1,8,1536]{3,2,1,0:T(8,128)} %param.20) | copy-start | bytes 147460
  113.7 165.2 %copy-start.4 = (f32[7]{0:T(128)S(1)}, f32[7]{0:T(128)}, u32[]{:S(2)}) copy-start(f32[7]{0:T(128)} %param.21) | copy-start | bytes 88
  113.7 162.0 %collective-permute-start.3 = (f32[7,3,1,1536]{3,0,2,1:T(8,128)S(1)}, f32[7,3,1,1536]{3,0,2,1:T(8,128)S(1)}, u32[]{:S(2)}, u32[]{:S(2)}) collective-permute-start(f32[7,3,1,1536]{3,0,2,1:T(8,128)S(1)} %get-tuple-element.58), channel_id=1, source_target_pairs={{0,1},{1,2},{2,3},{3,4},{4,5},{5,6},{6,7},{7,8},{8,9},{9,10},{10,1... | collective-permute-start | bytes 387080 | tf_op jit(solution)/shard_map/ppermute | solution.py:16
  275.7 0.7 copy-start.3
  279.0 11.9 %collective-permute-start.5 = (f32[7,1,8,1536]{3,0,2,1:T(8,128)S(1)}, f32[7,1,8,1536]{3,0,2,1:T(8,128)S(1)}, u32[]{:S(2)}, u32[]{:S(2)}) collective-permute-start(f32[7,1,8,1536]{3,0,2,1:T(8,128)S(1)} %multiply_multiply_fusion), channel_id=1, source_target_pairs={{32,0},{64,32},{96,64},{128,96},{160,128},{192,160},{224,192},{33,... | collective-permute-start | bytes 1032200 | tf_op jit(solution)/shard_map/ppermute | solution.py:19
  280.3 11.4 %collective-permute-start.6 = (f32[7,1,8,1536]{3,0,2,1:T(8,128)S(1)}, f32[7,1,8,1536]{3,0,2,1:T(8,128)S(1)}, u32[]{:S(2)}, u32[]{:S(2)}) collective-permute-start(f32[7,1,8,1536]{3,0,2,1:T(8,128)S(1)} %multiply_multiply_fusion), channel_id=1, source_target_pairs={{0,32},{32,64},{64,96},{96,128},{128,160},{160,192},{192,224},{1,3... | collective-permute-start | bytes 1032200 | tf_op jit(solution)/shard_map/ppermute | solution.py:16
  284.7 14.8 %collective-permute-start.9 = (f32[7,1,2,8]{3,2,0,1:T(2,128)S(1)}, f32[7,1,2,8]{3,2,0,1:T(2,128)S(1)}, u32[]{:S(2)}, u32[]{:S(2)}) collective-permute-start(f32[7,1,2,8]{3,2,0,1:T(2,128)S(1)} %pad_maximum_fusion.19), channel_id=1, source_target_pairs={{0,256},{256,0},{1,257},{257,1},{2,258},{258,2},{3,259},{259,3},{4... | collective-permute-start | bytes 1352 | tf_op jit(solution)/shard_map/ppermute | solution.py:8
  292.5 61.8 %collective-permute-start.7 = (f32[7,3,1,1536]{3,0,2,1:T(8,128)}, f32[7,3,1,1536]{3,0,2,1:T(8,128)}, u32[]{:S(2)}, u32[]{:S(2)}) collective-permute-start(f32[7,3,1,1536]{3,0,2,1:T(8,128)} %get-tuple-element.55), channel_id=1, source_target_pairs={{1,0},{2,1},{3,2},{4,3},{5,4},{6,5},{7,6},{8,7},{9,8},{10,9},{11,1... | collective-permute-start | bytes 387080 | tf_op jit(solution)/shard_map/ppermute | solution.py:19
  296.3 58.0 %collective-permute-start.8 = (f32[7,3,1,1536]{3,0,2,1:T(8,128)}, f32[7,3,1,1536]{3,0,2,1:T(8,128)}, u32[]{:S(2)}, u32[]{:S(2)}) collective-permute-start(f32[7,3,1,1536]{3,0,2,1:T(8,128)} %get-tuple-element.56), channel_id=1, source_target_pairs={{0,1},{1,2},{2,3},{3,4},{4,5},{5,6},{6,7},{7,8},{8,9},{9,10},{10,1... | collective-permute-start | bytes 387080 | tf_op jit(solution)/shard_map/ppermute | solution.py:16
Sparse Core Ops, SparseCore 0:
  111.0 154.9 all-reduce.5
where the time goes:
time: 365 us; the launch traced here: 364 us
  waiting for transfers between devices  151 us (41%)
  blocking collectives  69.8 us (19%)
  other arithmetic  64.2 us (18%)
  starting transfers between devices  42.5 us (12%)
  local copies, waits for them, and re-layouts  19.7 us (5%)
  between operations  13.8 us (4%)
    psum x1, waiting for transfers between devices, route_obs(): return lax.psum(dense, 'rad')  149 us
    all_gather x2, blocking collectives, other_edges(): return lax.all_gather(across, 'ang', axis=3, tiled=True)  69.8 us
    scatter-add x2, other arithmetic, ghost_terms(): target.at[:, :, flat_index]  31 us
    ppermute x4, starting transfers between devices, extended(): lax.ppermute(lax.slice_in_dim(block, block.shape[dim] - width, None, axis...  16.3 us
    scatter-add x1, other arithmetic, deposit(): return dense.at[:, cells].add(values, mode='drop')  14.8 us
    mul x1, other arithmetic, body(): forcing[moment].reshape(tile_rows, columns) * outer  9.62 us
    ppermute x2, starting transfers between devices, swapped(): lax.ppermute(x, axis, [(i, i ^ 1 << apart) for i in range(lax.axis_size(a...  9.26 us
    reshape x2, local copies, waits for them, and re-layouts, ghost_terms(): return target.reshape(fields, layers, central_rows, columns)  8.86 us
  transfers between devices with their start and end apart: 12, of which 3 were waited for; matrix products, arithmetic and copies ran while one was open for 22% of the time, Pallas kernels for 0%

commit v1 on v0

v1 whole, which is shorter than its diff:
```python
import functools
import jax
import jax.numpy as jnp
from jax import lax
from jax.experimental import pallas as pl
from jax.experimental.pallas import tpu as pltpu
from jax.sharding import PartitionSpec as P

MESH = pl.DeviceIdType.MESH
F32, BF16 = jnp.float32, jnp.bfloat16
FIELDS, ROWS, COLS = 7, 8, 1536
LANES = 128
BLOCKS = COLS // LANES
HIGH = ROWS * BLOCKS
LAYERS, TILES, GROUP = 8, 32, 4
LINES = TILES // GROUP
SLOTS = 16
POINTS = 4
OBS = 256
EDGE = TILES * ROWS
FORCED = 3

PIECES = ((0, 1), (11, 12), (1, 3), (3, 5), (5, 7), (7, 9), (9, 11))
GROUPS = ((0, 1), (2,), (3,), (4,), (5,), (6,))
ROW_PIECES = (((0, 12),), ((0, 1), (11, 12), (1, 5), (5, 9), (9, 11)))
ROW_AFTER = {0: (0, 1), 2: (2,), 4: (3,), 5: (4,)}


def iota(shape, dim, dtype=jnp.int32):
    value = lax.broadcasted_iota(jnp.int32, shape, dim)
    return value if dtype == jnp.int32 else value.astype(dtype)


def dot_rows(a, b, precision=None):
    return lax.dot_general(
        a, b, (((1,), (1,)), ((), ())), precision=precision, preferred_element_type=F32
    )


def two_parts(row):
    wide = jnp.broadcast_to(row, (16, row.shape[1]))
    high = wide.astype(BF16)
    low = (wide - high.astype(F32)).astype(BF16)
    return high, low


def spread(onehot_high, row):
    count, width = onehot_high.shape
    grid = onehot_high.reshape(count // 16, 16, width)
    return [(grid * part[None]).reshape(count, width) for part in two_parts(row)]


def kernel(
    adj, cond, diffus, couple, ghost_row, ghost_col, ghost_wt, dest, cell, obs_wt, misfit,
    out,
    scaled_a, scaled_b, base, layer_in, row_out, row_in,
    edge_out, edge_in, edge_sum, edge_all, edge_rows,
    high_hot, low_hot,
    outbox, line_in, pair_sum, tile_in, forced_in, forcing,
    layer_ss, layer_rs, row_ss, row_rs,
    edge_ss, edge_rs, line_ss, line_rs,
    obs1_ss, obs1_rs, obs2_ss, obs2_rs, obs3_ss, obs3_rs,
):
    p, z, a = lax.axis_index("panel"), lax.axis_index("rad"), lax.axis_index("ang")
    y, q = a // GROUP, lax.rem(a, GROUP)
    has_low, has_high = z > 0, z < LAYERS - 1
    has_north, has_south = a > 0, a < TILES - 1
    outer = z == LAYERS - 1
    inner = z < LAYERS - 1
    scaled = (scaled_a, scaled_b)

    def along_line(step):
        return lax.rem(y + step, LINES)

    def beside(step):
        return lax.rem(q + step, GROUP)

    barrier = pltpu.get_barrier_semaphore()

    def greet(panel, layer, tile):
        pl.semaphore_signal(barrier, inc=1, device_id=(panel, layer, tile), device_id_type=MESH)

    @pl.when(has_low)
    def _():
        greet(p, z - 1, a)

    @pl.when(has_high)
    def _():
        greet(p, z + 1, a)

    @pl.when(has_north)
    def _():
        greet(p, z, a - 1)

    @pl.when(has_south)
    def _():
        greet(p, z, a + 1)

    for i in range(GROUP):
        greet(1 - p, z, y * GROUP + i)
    for i in range(1, LINES):
        greet(p, z, along_line(i) * GROUP + q)
    for i in range(1, GROUP):
        greet(p, z, y * GROUP + beside(i))

    @pl.when(outer)
    def _():
        for i in range(LAYERS - 1):
            greet(p, i, a)

    def layer_copy(step, way, piece):
        start, stop = PIECES[piece]
        cols = slice(start * LANES, stop * LANES)
        return pltpu.make_async_remote_copy(
            src_ref=scaled[step].at[:, :, cols],
            dst_ref=layer_in.at[step, way, :, :, cols],
            send_sem=layer_ss.at[step, way, piece],
            recv_sem=layer_rs.at[step, way, piece],
            device_id=(p, z + 1 if way == 0 else z - 1, a),
            device_id_type=MESH,
        )

    def row_copy(step, way, piece):
        start, stop = ROW_PIECES[step][piece]
        cols = slice(start * LANES, stop * LANES)
        return pltpu.make_async_remote_copy(
            src_ref=row_out.at[step, way, :, cols],
            dst_ref=row_in.at[step, way, :, cols],
            send_sem=row_ss.at[step, way, piece],
            recv_sem=row_rs.at[step, way, piece],
            device_id=(p, z, a + 1 if way == 0 else a - 1),
            device_id_type=MESH,
        )

    def edge_copy(step, i, origin):
        return pltpu.make_async_remote_copy(
            src_ref=edge_out.at[step],
            dst_ref=edge_in.at[step, origin],
            send_sem=edge_ss.at[step, i],
            recv_sem=edge_rs.at[step, origin],
            device_id=(1 - p, z, y * GROUP + i),
            device_id_type=MESH,
        )

    def line_copy(step, i, origin):
        return pltpu.make_async_remote_copy(
            src_ref=edge_sum.at[step],
            dst_ref=edge_all.at[step, origin],
            send_sem=line_ss.at[step, i],
            recv_sem=line_rs.at[step, origin],
            device_id=(p, z, along_line(i) * GROUP + q),
            device_id_type=MESH,
        )

    def obs1_copy(i, origin):
        target = along_line(i)
        return pltpu.make_async_remote_copy(
            src_ref=outbox.at[pl.ds(target * GROUP, GROUP)],
            dst_ref=line_in.at[origin],
            send_sem=obs1_ss.at[i],
            recv_sem=obs1_rs.at[origin],
            device_id=(p, z, target * GROUP + q),
            device_id_type=MESH,
        )

    def obs2_copy(i, origin):
        target = beside(i)
        return pltpu.make_async_remote_copy(
            src_ref=pair_sum.at[target],
            dst_ref=tile_in.at[origin],
            send_sem=obs2_ss.at[i],
            recv_sem=obs2_rs.at[origin],
            device_id=(p, z, y * GROUP + target),
            device_id_type=MESH,
        )

    def obs3_copy(origin):
        return pltpu.make_async_remote_copy(
            src_ref=tile_in,
            dst_ref=forced_in.at[origin],
            send_sem=obs3_ss.at[0],
            recv_sem=obs3_rs.at[origin],
            device_id=(p, LAYERS - 1, a),
            device_id_type=MESH,
        )

    def send_layers(step, piece):
        @pl.when(has_high)
        def _():
            layer_copy(step, 0, piece).start()

        @pl.when(has_low)
        def _():
            layer_copy(step, 1, piece).start()

    def take_layers(step, piece):
        @pl.when(has_low)
        def _():
            layer_copy(step, 0, piece).wait_recv()

        @pl.when(has_high)
        def _():
            layer_copy(step, 1, piece).wait_recv()

    def send_rows(step, piece):
        @pl.when(has_south)
        def _():
            row_copy(step, 0, piece).start()

        @pl.when(has_north)
        def _():
            row_copy(step, 1, piece).start()

    def take_rows(step, piece):
        @pl.when(has_north)
        def _():
            row_copy(step, 0, piece).wait_recv()

        @pl.when(has_south)
        def _():
            row_copy(step, 1, piece).wait_recv()

    lane_of = iota((ROWS, LANES), 1)
    own_lane = lane_of == lax.rem(a, LANES // ROWS) * ROWS + iota((ROWS, LANES), 0)

    def fill_edges(step):
        for f in range(FIELDS):
            for side in range(2):
                block = scaled[step][f, :, (0 if side == 0 else COLS - LANES):(LANES if side == 0 else COLS)]
                column = block[:, 0:1] if side == 0 else block[:, LANES - 1:LANES]
                wide = jnp.where(own_lane, jnp.broadcast_to(column, (ROWS, LANES)), 0.0)
                edge_out[step, side, f:f + 1, :] = jnp.sum(wide, axis=0, keepdims=True)

    def fill_base(step, source, target):
        rate = [[couple[e, c] for c in range(FIELDS)] for e in range(FIELDS)]
        for b in range(BLOCKS):
            cols = slice(b * LANES, (b + 1) * LANES)
            state = [source[e, :, cols] for e in range(FIELDS)]
            for c in range(FIELDS):
                total = state[c]
                for e in range(FIELDS):
                    total = total + rate[e][c] * state[e]
                target[c, :, cols] = total
        col_of = iota((ROWS, COLS), 1)
        row_of = iota((ROWS, COLS), 0)
        for f in range(FIELDS):
            s = scaled[step][f]
            west = jnp.where(col_of == 0, 0.0, pltpu.roll(s, 1, 1))
            east = jnp.where(col_of == COLS - 1, 0.0, pltpu.roll(s, COLS - 1, 1))
            north = jnp.where(row_of == 0, 0.0, pltpu.roll(s, 1, 0))
            south = jnp.where(row_of == ROWS - 1, 0.0, pltpu.roll(s, ROWS - 1, 0))
            target[f] = target[f] + ((west + east) + (north + south) - 6.0 * s)

    def forward_edges(step):
        for i in range(GROUP):
            edge_copy(step, i, i).wait_recv()
        total = edge_in[step, 0] + edge_in[step, 1] + edge_in[step, 2] + edge_in[step, 3]
        edge_sum[step] = total
        edge_all[step, y] = total
        for i in range(1, LINES):
            line_copy(step, i, y).start()

    def add_ghost(step, target):
        for i in range(1, LINES):
            line_copy(step, i, along_line(i)).wait_recv()
        half = LINES // 2
        for side in range(2):
            for h in range(2):
                total = edge_all[step, h * half, side]
                for i in range(1, half):
                    total = total + edge_all[step, h * half + i, side]
                edge_rows[side, 0:FIELDS, h * LANES:(h + 1) * LANES] = total

        def one_field(f, carry):
            rows = []
            for side in range(2):
                edge = edge_rows[side, pl.ds(f, 1), :]
                for point in range(POINTS):
                    rows.append(edge * ghost_wt[side, point:point + 1, :])
            high, low = spread(high_hot[...], jnp.concatenate(rows, axis=1))
            cells = dot_rows(high, low_hot[...]) + dot_rows(low, low_hot[...])
            for b in range(BLOCKS):
                cols = slice(b * LANES, (b + 1) * LANES)
                target[f, :, cols] = target[f, :, cols] + cells[b * ROWS:(b + 1) * ROWS]
            return carry

        lax.fori_loop(0, FIELDS, one_field, 0)

    for f in range(FIELDS):
        value = (diffus[f] * cond[...]) * adj[f]
        scaled_a[f] = value
        row_out[0, 0, f:f + 1, :] = value[ROWS - 1:ROWS]
        row_out[0, 1, f:f + 1, :] = value[0:1]
    fill_edges(0)

    for step in range(2):
        @pl.when(jnp.logical_not(has_low))
        def _():
            layer_in[step, 0] = jnp.zeros((FIELDS, ROWS, COLS), F32)

        @pl.when(jnp.logical_not(has_high))
        def _():
            layer_in[step, 1] = jnp.zeros((FIELDS, ROWS, COLS), F32)

        @pl.when(jnp.logical_not(has_north))
        def _():
            row_in[step, 0] = jnp.zeros((FIELDS, COLS), F32)

        @pl.when(jnp.logical_not(has_south))
        def _():
            row_in[step, 1] = jnp.zeros((FIELDS, COLS), F32)

    def count(flag):
        return jnp.where(flag, 1, 0)

    expected = (
        GROUP + LINES - 1 + GROUP - 1
        + count(has_low) + count(has_high) + count(has_north) + count(has_south) + count(inner)
    )
    pl.semaphore_wait(barrier, expected)

    for i in range(GROUP):
        edge_copy(0, i, q).start()
    send_rows(0, 0)
    for piece in range(len(PIECES)):
        send_layers(0, piece)

    owner_hot = jnp.where(iota((TILES, OBS), 0) == dest[...], 1.0, 0.0)
    earlier = jnp.where(iota((OBS, OBS), 1) < iota((OBS, OBS), 0), 1.0, 0.0).astype(BF16)
    before = dot_rows(owner_hot.astype(BF16), earlier)
    rank = jnp.sum(owner_hot * before, axis=0, keepdims=True)
    in_slot = rank == iota((SLOTS, OBS), 0, F32)
    number = cell[...]
    in_row = jnp.floor((number.astype(F32) + 0.5) * (1.0 / COLS)).astype(jnp.int32)
    column = number - in_row * COLS
    place = ((lax.shift_right_logical(column, 7) * ROWS + in_row) * LANES + (column & (LANES - 1))).astype(F32)
    payload = []
    for kind in range(3):
        for point in range(POINTS):
            if kind < 2:
                row = misfit[kind:kind + 1, :] * obs_wt[point:point + 1, :]
            else:
                row = place[point:point + 1, :]
            payload.append(jnp.where(in_slot, jnp.broadcast_to(row, (SLOTS, OBS)), 0.0))
    packed = dot_rows(owner_hot, jnp.concatenate(payload, axis=0), lax.Precision.HIGHEST)
    width = SLOTS * POINTS
    own_half = iota((TILES, LANES), 1) // width == lax.rem(y, 2)
    for kind in range(3):
        part = packed[:, kind * width:(kind + 1) * width]
        outbox[:, kind, :] = jnp.where(own_half, jnp.concatenate([part, part], axis=1), 0.0)
    outbox[:, 3, :] = jnp.zeros((TILES, LANES), F32)
    for i in range(1, LINES):
        obs1_copy(i, y).start()
    line_in[y] = outbox[pl.ds(y * GROUP, GROUP)]

    fill_base(0, adj, base)

    for side in range(2):
        for point in range(POINTS):
            at = (side * POINTS + point) * EDGE
            local = ghost_row[side, point:point + 1, :] - a * ROWS
            col = ghost_col[side, point:point + 1, :]
            inside = (local >= 0) & (local < ROWS)
            high = jnp.where(inside, lax.shift_right_logical(col, 7) * ROWS + local, -1)
            low = col & (LANES - 1)
            high_hot[:, at:at + EDGE] = jnp.where(iota((HIGH, EDGE), 0) == high, 1.0, 0.0).astype(BF16)
            low_hot[:, at:at + EDGE] = jnp.where(iota((LANES, EDGE), 0) == low, 1.0, 0.0).astype(BF16)

    forward_edges(0)

    for i in range(1, LINES):
        obs1_copy(i, along_line(i)).wait_recv()
    for i in range(GROUP):
        for pair in range(LINES // 2):
            pair_sum[i, pair] = line_in[2 * pair, i] + line_in[2 * pair + 1, i]
    for i in range(1, GROUP):
        obs2_copy(i, q).start()
    tile_in[q] = pair_sum[q]

    add_ghost(0, base)

    for i in range(1, GROUP):
        obs2_copy(i, beside(i)).wait_recv()

    @pl.when(inner)
    def _():
        obs3_copy(z).start()

    @pl.when(outer)
    def _():
        forced_in[LAYERS - 1] = tile_in[...]
        for i in range(LAYERS - 1):
            obs3_copy(i).wait_recv()
        forcing[...] = jnp.zeros((2, HIGH, LANES), F32)

        def one_layer(layer, carry):
            rows = [[], [], []]
            for i in range(GROUP):
                for pair in range(LINES // 2):
                    for kind in range(3):
                        rows[kind].append(forced_in[layer, i, pair, kind:kind + 1, :])
            first_time, second_time, places = [jnp.concatenate(r, axis=1) for r in rows]
            high = jnp.floor(places * (1.0 / LANES))
            low = places - high * LANES
            size = places.shape[1]
            hot_high = jnp.where(iota((HIGH, size), 0, F32) == high, 1.0, 0.0).astype(BF16)
            hot_low = jnp.where(iota((LANES, size), 0, F32) == low, 1.0, 0.0).astype(BF16)
            for moment, row in enumerate((first_time, second_time)):
                top, rest = spread(hot_high, row)
                forcing[moment] = forcing[moment] + (dot_rows(top, hot_low) + dot_rows(rest, hot_low))
            return carry

        lax.fori_loop(0, LAYERS, one_layer, 0)
        for b in range(BLOCKS):
            cols = slice(b * LANES, (b + 1) * LANES)
            base[FORCED, :, cols] = base[FORCED, :, cols] + forcing[1, b * ROWS:(b + 1) * ROWS]

    def with_halos(value, step, f, cols):
        size = cols.stop - cols.start
        row_of = iota((ROWS, size), 0)
        value = value + (layer_in[step, 0, f, :, cols] + layer_in[step, 1, f, :, cols])
        north = jnp.broadcast_to(row_in[step, 0, f:f + 1, cols], (ROWS, size))
        south = jnp.broadcast_to(row_in[step, 1, f:f + 1, cols], (ROWS, size))
        return value + jnp.where(row_of == 0, north, jnp.where(row_of == ROWS - 1, south, 0.0))

    take_rows(0, 0)
    for g, group in enumerate(GROUPS):
        for piece in group:
            take_layers(0, piece)
            start, stop = PIECES[piece]
            cols = slice(start * LANES, stop * LANES)
            for f in range(FIELDS):
                value = with_halos(base[f, :, cols], 0, f, cols)
                base[f, :, cols] = value
                value = (diffus[f] * cond[:, cols]) * value
                scaled_b[f, :, cols] = value
                row_out[1, 0, f:f + 1, cols] = value[ROWS - 1:ROWS]
                row_out[1, 1, f:f + 1, cols] = value[0:1]
            send_layers(1, piece)
        for piece in ROW_AFTER.get(g, ()):
            send_rows(1, piece)
        if g == 0:
            fill_edges(1)
            for i in range(GROUP):
                edge_copy(1, i, q).start()

    forward_edges(1)
    fill_base(1, base, out)
    add_ghost(1, out)

    @pl.when(outer)
    def _():
        for b in range(BLOCKS):
            cols = slice(b * LANES, (b + 1) * LANES)
            out[FORCED, :, cols] = out[FORCED, :, cols] + forcing[0, b * ROWS:(b + 1) * ROWS]

    for piece in range(len(ROW_PIECES[1])):
        take_rows(1, piece)
    for piece, (start, stop) in enumerate(PIECES):
        take_layers(1, piece)
        cols = slice(start * LANES, stop * LANES)
        for f in range(FIELDS):
            out[f, :, cols] = with_halos(out[f, :, cols], 1, f, cols)

    for step in range(2):
        for i in range(GROUP):
            edge_copy(step, i, q).wait_send()
        for i in range(1, LINES):
            line_copy(step, i, y).wait_send()
    for i in range(1, LINES):
        obs1_copy(i, y).wait_send()
    for i in range(1, GROUP):
        obs2_copy(i, q).wait_send()

    @pl.when(inner)
    def _():
        obs3_copy(z).wait_send()

    for step in range(2):
        for way, flag in ((0, has_high), (1, has_low)):
            @pl.when(flag)
            def _():
                for piece in range(len(PIECES)):
                    layer_copy(step, way, piece).wait_send()

        for way, flag in ((0, has_south), (1, has_north)):
            @pl.when(flag)
            def _():
                for piece in range(len(ROW_PIECES[step])):
                    row_copy(step, way, piece).wait_send()


def steps(*operands):
    vmem = pl.BlockSpec(memory_space=pltpu.VMEM)
    smem = pl.BlockSpec(memory_space=pltpu.SMEM)
    dma = pltpu.SemaphoreType.DMA
    state = (FIELDS, ROWS, COLS)
    terms = 2 * POINTS * EDGE
    pieces, row_pieces = len(PIECES), max(len(r) for r in ROW_PIECES)
    pairs = LINES // 2
    return pl.pallas_call(
        kernel,
        out_shape=jax.ShapeDtypeStruct(state, F32),
        in_specs=[vmem, vmem, smem, smem] + [vmem] * 7,
        out_specs=vmem,
        scratch_shapes=[
            pltpu.VMEM(state, F32),
            pltpu.VMEM(state, F32),
            pltpu.VMEM(state, F32),
            pltpu.VMEM((2, 2) + state, F32),
            pltpu.VMEM((2, 2, FIELDS, COLS), F32),
            pltpu.VMEM((2, 2, FIELDS, COLS), F32),
            pltpu.VMEM((2, 2, FIELDS, LANES), F32),
            pltpu.VMEM((2, GROUP, 2, FIELDS, LANES), F32),
            pltpu.VMEM((2, 2, FIELDS, LANES), F32),
            pltpu.VMEM((2, LINES, 2, FIELDS, LANES), F32),
            pltpu.VMEM((2, 8, EDGE), F32),
            pltpu.VMEM((HIGH, terms), BF16),
            pltpu.VMEM((LANES, terms), BF16),
            pltpu.VMEM((TILES, 4, LANES), F32),
            pltpu.VMEM((LINES, GROUP, 4, LANES), F32),
            pltpu.VMEM((GROUP, pairs, 4, LANES), F32),
            pltpu.VMEM((GROUP, pairs, 4, LANES), F32),
            pltpu.VMEM((LAYERS, GROUP, pairs, 4, LANES), F32),
            pltpu.VMEM((2, HIGH, LANES), F32),
            dma((2, 2, pieces)), dma((2, 2, pieces)),
            dma((2, 2, row_pieces)), dma((2, 2, row_pieces)),
            dma((2, GROUP)), dma((2, GROUP)),
            dma((2, LINES)), dma((2, LINES)),
            dma((LINES,)), dma((LINES,)),
            dma((GROUP,)), dma((GROUP,)),
            dma((1,)), dma((LAYERS,)),
        ],
        compiler_params=pltpu.CompilerParams(
            collective_id=0, has_side_effects=True, vmem_limit_bytes=40 << 20
        ),
        name="adjoint_steps",
    )(*operands)


def body(
    adj_final, cond, diffus, couple, ghost_row, ghost_col, ghost_wt, obs_dest, obs_cell, obs_wt,
    misfit,
):
    final = steps(
        adj_final.reshape(FIELDS, ROWS, COLS), cond[0, 0], diffus, couple, ghost_row, ghost_col,
        ghost_wt, obs_dest.reshape(1, OBS), obs_cell[0, 0], obs_wt[0, 0], misfit[0, 0],
    )
    return final[None, :, None]


def solution(mesh):
    placed = (
        P("panel", None, "rad", "ang", None),
        P("panel", "rad", "ang", None),
        P(),
        P(),
        P(),
        P(),
        P(),
        P("panel", "rad", "ang", None),
        P("panel", "rad", None, "ang"),
        P("panel", "rad", None, "ang"),
        P("panel", "rad", None, "ang"),
    )
    return jax.shard_map(
        body,
        mesh=mesh,
        in_specs=placed,
        out_specs=P("panel", None, "rad", "ang", None),
        check_vma=False,
    )
```

time: 365 us -> 51.3 us (0.14)
  the two profiles are of different devices: /device:TPU:1 before, /device:TPU:448 now
where the time goes in v1:
time: 51.3 us; the launch traced here: 50.8 us
  Pallas kernels  43.5 us (85%)
  local copies, waits for them, and re-layouts  7.32 us (14%)
    pallas_call x1, Pallas kernels, steps(): pl.pallas_call(kernel, out_shape=jax.ShapeDtypeStruct(state, F32), in_spe...  43.5 us
    unnamed x23, local copies, waits for them, and re-layouts  7.32 us

profile of v1, /device:TPU:448, one launch (start us, length us, event | category | flops | bytes accessed | tf_op | source)
XLA Modules:
  0.0 50.8 jit_solution(7014207529217509057)
XLA Ops:
  0.0 0.0 copy-start.2
  0.0 0.0 copy-start.8
  0.0 0.0 copy-start.9
  0.0 0.7 %copy-done.2 = s32[2,4,256]{2,1,0:T(4,128)S(1)} copy-done((s32[2,4,256]{2,1,0:T(4,128)S(1)}, s32[2,4,256]{2,1,0:T(4,128)}, u32[]{:S(2)}) %copy-start.2) | copy-done | bytes 8216
  0.7 0.0 copy-done.8
  0.7 0.0 copy-done.9
  0.7 0.0 copy-start
  0.7 1.0 %copy-done = f32[1,7,1,8,1536]{4,3,2,1,0:T(8,128)S(1)} copy-done((f32[1,7,1,8,1536]{4,3,2,1,0:T(8,128)S(1)}, f32[1,7,1,8,1536]{4,3,2,1,0:T(8,128)}, u32[]{:S(2)}) %copy-start) | copy-done | bytes 344088
  1.7 0.0 copy-start.1
  1.7 0.8 %copy-done.1 = f32[1,1,8,1536]{3,2,1,0:T(8,128)S(1)} copy-done((f32[1,1,8,1536]{3,2,1,0:T(8,128)S(1)}, f32[1,1,8,1536]{3,2,1,0:T(8,128)}, u32[]{:S(2)}) %copy-start.1) | copy-done | bytes 49176
  2.5 0.0 copy-start.3
  2.5 0.7 %copy-done.3 = s32[2,4,256]{2,1,0:T(4,128)S(1)} copy-done((s32[2,4,256]{2,1,0:T(4,128)S(1)}, s32[2,4,256]{2,1,0:T(4,128)}, u32[]{:S(2)}) %copy-start.3) | copy-done | bytes 8216
  3.2 0.0 copy-start.4
  3.2 0.7 %copy-done.4 = f32[2,4,256]{2,1,0:T(4,128)S(1)} copy-done((f32[2,4,256]{2,1,0:T(4,128)S(1)}, f32[2,4,256]{2,1,0:T(4,128)}, u32[]{:S(2)}) %copy-start.4) | copy-done | bytes 8216
  3.9 0.0 copy-start.5
  3.9 0.7 %copy-done.5 = f32[7,7]{1,0:T(8,128)S(1)} copy-done((f32[7,7]{1,0:T(8,128)S(1)}, f32[7,7]{1,0:T(8,128)}, u32[]{:S(2)}) %copy-start.5) | copy-done | bytes 220
  4.6 0.0 copy-start.6
  4.6 0.7 %copy-done.6 = s32[1,1,4,256]{3,2,1,0:T(4,128)S(1)} copy-done((s32[1,1,4,256]{3,2,1,0:T(4,128)S(1)}, s32[1,1,4,256]{3,2,1,0:T(4,128)}, u32[]{:S(2)}) %copy-start.6) | copy-done | bytes 4120
  5.3 0.0 copy-start.7
  5.3 0.7 %copy-done.7 = f32[1,1,4,256]{3,2,1,0:T(4,128)S(1)} copy-done((f32[1,1,4,256]{3,2,1,0:T(4,128)S(1)}, f32[1,1,4,256]{3,2,1,0:T(4,128)}, u32[]{:S(2)}) %copy-start.7) | copy-done | bytes 4120
  5.9 0.0 copy-start.10
  5.9 0.7 %copy-done.10 = f32[7]{0:T(128)S(1)} copy-done((f32[7]{0:T(128)S(1)}, f32[7]{0:T(128)}, u32[]{:S(2)}) %copy-start.10) | copy-done | bytes 52
  6.6 43.5 %adjoint_steps.1 = f32[7,8,1536]{2,1,0:T(8,128)S(1)} custom-call(f32[7,8,1536]{2,1,0:T(8,128)S(1)} %bitcast.10, f32[8,1536]{1,0:T(8,128)S(1)} %bitcast.11, f32[7]{0:T(128)S(1)} %copy-done.10, f32[7,7]{1,0:T(8,128)S(1)} %copy-done.5, s32[2,4,256]{2,1,0:T(4,128)S(1)} %copy-done.2, s32[2,4,256]{2,1,0:T(4,128)S(1)} %copy-done.3, f32[2,4,256]{2,1,0:T(4,128)S(1)} %copy-done.4, ...), custom_call_target="tpu_custom_call" | custom-call | tf_op jit(solution)/shard_map/adjoint_steps/pallas_call | solution.py:501
  50.1 0.7 %copy.14 = f32[1,7,1,8,1536]{4,3,2,1,0:T(8,128)} copy(f32[1,7,1,8,1536]{4,3,2,1,0:T(8,128)S(1)} %bitcast.9) | data formatting | bytes 688128
Async XLA Ops:
  0.0 0.7 %copy-start.2 = (s32[2,4,256]{2,1,0:T(4,128)S(1)}, s32[2,4,256]{2,1,0:T(4,128)}, u32[]{:S(2)}) copy-start(s32[2,4,256]{2,1,0:T(4,128)} %ghost_row.1) | copy-start | bytes 24580
  0.0 0.7 %copy-start.8 = (f32[1,1,2,256]{3,2,1,0:T(2,128)S(1)}, f32[1,1,2,256]{3,2,1,0:T(2,128)}, u32[]{:S(2)}) copy-start(f32[1,1,2,256]{3,2,1,0:T(2,128)} %param.21) | copy-start | bytes 6148
  0.0 0.7 %copy-start.9 = (s32[1,1,256,1]{2,3,1,0:T(1,128)S(1)}, s32[1,1,256,1]{2,3,1,0:T(1,128)}, u32[]{:S(2)}) copy-start(s32[1,1,256,1]{2,3,1,0:T(1,128)} %param.18) | copy-start | bytes 3076
  0.7 1.0 %copy-start = (f32[1,7,1,8,1536]{4,3,2,1,0:T(8,128)S(1)}, f32[1,7,1,8,1536]{4,3,2,1,0:T(8,128)}, u32[]{:S(2)}) copy-start(f32[1,7,1,8,1536]{4,3,2,1,0:T(8,128)} %param.11) | copy-start | bytes 1032196
  1.7 0.8 %copy-start.1 = (f32[1,1,8,1536]{3,2,1,0:T(8,128)S(1)}, f32[1,1,8,1536]{3,2,1,0:T(8,128)}, u32[]{:S(2)}) copy-start(f32[1,1,8,1536]{3,2,1,0:T(8,128)} %param.12) | copy-start | bytes 147460
  2.5 0.7 %copy-start.3 = (s32[2,4,256]{2,1,0:T(4,128)S(1)}, s32[2,4,256]{2,1,0:T(4,128)}, u32[]{:S(2)}) copy-start(s32[2,4,256]{2,1,0:T(4,128)} %ghost_col.1) | copy-start | bytes 24580
  3.2 0.7 %copy-start.4 = (f32[2,4,256]{2,1,0:T(4,128)S(1)}, f32[2,4,256]{2,1,0:T(4,128)}, u32[]{:S(2)}) copy-start(f32[2,4,256]{2,1,0:T(4,128)} %ghost_wt.1) | copy-start | bytes 24580
  3.9 0.7 %copy-start.5 = (f32[7,7]{1,0:T(8,128)S(1)}, f32[7,7]{1,0:T(8,128)}, u32[]{:S(2)}) copy-start(f32[7,7]{1,0:T(8,128)} %couple.1) | copy-start | bytes 592
  4.6 0.7 %copy-start.6 = (s32[1,1,4,256]{3,2,1,0:T(4,128)S(1)}, s32[1,1,4,256]{3,2,1,0:T(4,128)}, u32[]{:S(2)}) copy-start(s32[1,1,4,256]{3,2,1,0:T(4,128)} %param.19) | copy-start | bytes 12292
  5.3 0.7 %copy-start.7 = (f32[1,1,4,256]{3,2,1,0:T(4,128)S(1)}, f32[1,1,4,256]{3,2,1,0:T(4,128)}, u32[]{:S(2)}) copy-start(f32[1,1,4,256]{3,2,1,0:T(4,128)} %param.20) | copy-start | bytes 12292
  5.9 0.7 %copy-start.10 = (f32[7]{0:T(128)S(1)}, f32[7]{0:T(128)}, u32[]{:S(2)}) copy-start(f32[7]{0:T(128)} %diffus.1) | copy-start | bytes 88

commit v2 on v1

v2 whole, which is shorter than its diff:
```python
import functools
import jax
import jax.numpy as jnp
from jax import lax
from jax.experimental import pallas as pl
from jax.experimental.pallas import tpu as pltpu
from jax.sharding import PartitionSpec as P

MESH = pl.DeviceIdType.MESH
F32, BF16 = jnp.float32, jnp.bfloat16
FIELDS, ROWS, COLS = 7, 8, 1536
LANES = 128
BLOCKS = COLS // LANES
WIDE = 256
SPANS = COLS // WIDE
HIGH = ROWS * SPANS
LAYERS, TILES, GROUP = 8, 32, 4
LINES = TILES // GROUP
SLOTS = 16
POINTS = 4
OBS = 256
EDGE = TILES * ROWS
FORCED = 3

PIECES = ((0, 512), (512, 1024), (1024, 1536))


def iota(shape, dim, dtype=jnp.int32):
    value = lax.broadcasted_iota(jnp.int32, shape, dim)
    return value if dtype == jnp.int32 else value.astype(dtype)


def dot_rows(a, b, precision=None):
    return lax.dot_general(
        a, b, (((1,), (1,)), ((), ())), precision=precision, preferred_element_type=F32
    )


def indicator(count, row):
    small = row.astype(BF16)
    hot = iota((count, row.shape[1]), 0, F32).astype(BF16) == jnp.broadcast_to(small, (count, row.shape[1]))
    return jnp.where(hot, jnp.ones((), BF16), jnp.zeros((), BF16))


def spread(high_hot, row):
    count, width = high_hot.shape
    wide = jnp.broadcast_to(row, (16, width))
    top = wide.astype(BF16)
    rest = (wide - top.astype(F32)).astype(BF16)
    grid = high_hot.reshape(count // 16, 16, width)
    return [(grid * part[None]).reshape(count, width) for part in (top, rest)]


def kernel(
    adj_hbm, cond_hbm, diffus_hbm, couple_hbm, ghost_row_hbm, ghost_col_hbm, ghost_wt_hbm,
    dest_hbm, cell_hbm, obs_wt_hbm, misfit_hbm,
    out,
    adj, cond, diffus, couple, ghost_row, ghost_col, ghost_wt, dest, cell, obs_wt, misfit, load_s,
    scaled_a, scaled_b, scaled_f, base, layer_in, row_out, row_in,
    edge_out, edge_in, edge_sum, edge_all, edge_rows,
    high_hot, low_hot, spread_rows,
    outbox, line_in, pair_sum, tile_in, forced_in, forcing, late_out, late_in,
    layer_ss, layer_rs, row_ss, row_rs,
    edge_ss, edge_rs, line_ss, line_rs, obs_ss, obs_rs, late_ss, late_rs,
):
    loads = [
        pltpu.make_async_copy(source, target, load_s.at[i])
        for i, (source, target) in enumerate((
            (adj_hbm, adj), (cond_hbm, cond), (diffus_hbm, diffus), (couple_hbm, couple),
            (dest_hbm, dest), (cell_hbm, cell), (obs_wt_hbm, obs_wt), (misfit_hbm, misfit),
            (ghost_row_hbm, ghost_row), (ghost_col_hbm, ghost_col), (ghost_wt_hbm, ghost_wt),
        ))
    ]
    for load in loads[:3]:
        load.start()

    p, z, a = lax.axis_index("panel"), lax.axis_index("rad"), lax.axis_index("ang")
    y, q = a // GROUP, lax.rem(a, GROUP)
    has_low, has_high = z > 0, z < LAYERS - 1
    has_north, has_south = a > 0, a < TILES - 1
    outer = z == LAYERS - 1
    inner = z < LAYERS - 1
    scaled = (scaled_a, scaled_b)

    def along_line(step):
        return lax.rem(y + step, LINES)

    def beside(step):
        return lax.rem(q + step, GROUP)

    barrier = pltpu.get_barrier_semaphore()

    def greet(panel, layer, tile):
        pl.semaphore_signal(barrier, inc=1, device_id=(panel, layer, tile), device_id_type=MESH)

    @pl.when(has_low)
    def _():
        greet(p, z - 1, a)

    @pl.when(has_high)
    def _():
        greet(p, z + 1, a)

    @pl.when(has_north)
    def _():
        greet(p, z, a - 1)

    @pl.when(has_south)
    def _():
        greet(p, z, a + 1)

    for i in range(GROUP):
        greet(1 - p, z, y * GROUP + i)
    for i in range(1, LINES):
        greet(p, z, along_line(i) * GROUP + q)
    for i in range(1, GROUP):
        greet(p, z, y * GROUP + beside(i))

    @pl.when(outer)
    def _():
        for i in range(LAYERS - 1):
            greet(p, i, a)

    for load in loads[3:]:
        load.start()

    def remote(source, target, send, recv, device):
        return pltpu.make_async_remote_copy(
            src_ref=source, dst_ref=target, send_sem=send, recv_sem=recv,
            device_id=device, device_id_type=MESH,
        )

    def layer_copy(step, way, start=0, stop=COLS, piece=0):
        return remote(
            scaled[step].at[:, :, start:stop], layer_in.at[step, way, :, :, start:stop],
            layer_ss.at[step, way], layer_rs.at[step, way, piece],
            (p, z + 1 if way == 0 else z - 1, a),
        )

    def row_copy(step, way):
        return remote(
            row_out.at[step, way], row_in.at[step, way], row_ss.at[step, way], row_rs.at[step, way],
            (p, z, a + 1 if way == 0 else a - 1),
        )

    def edge_copy(step, i):
        return remote(
            edge_out.at[step], edge_in.at[step, q], edge_ss.at[step], edge_rs.at[step],
            (1 - p, z, y * GROUP + i),
        )

    def edges_moved(step):
        everything = edge_in.at[step]
        return remote(everything, everything, edge_ss.at[step], edge_rs.at[step], (1 - p, z, a))

    def line_copy(step, i):
        return remote(
            edge_sum.at[step], edge_all.at[step, y], line_ss.at[step], line_rs.at[step],
            (p, z, along_line(i) * GROUP + q),
        )

    def lines_moved(step):
        others = edge_all.at[step, pl.ds(0, LINES - 1)]
        return remote(others, others, line_ss.at[step], line_rs.at[step], (1 - p, z, a))

    def obs1_copy(i):
        target = along_line(i)
        return remote(
            outbox.at[pl.ds(target * GROUP, GROUP)], line_in.at[y], obs_ss.at[0], obs_rs.at[0],
            (p, z, target * GROUP + q),
        )

    def obs1_moved():
        others = line_in.at[pl.ds(0, LINES - 1)]
        return remote(others, others, obs_ss.at[0], obs_rs.at[0], (1 - p, z, a))

    def obs2_copy(i):
        target = beside(i)
        return remote(
            pair_sum.at[target], tile_in.at[q], obs_ss.at[1], obs_rs.at[1],
            (p, z, y * GROUP + target),
        )

    def obs2_moved():
        others = tile_in.at[pl.ds(0, GROUP - 1)]
        return remote(others, others, obs_ss.at[1], obs_rs.at[1], (1 - p, z, a))

    def obs3_copy():
        return remote(tile_in, forced_in.at[z], obs_ss.at[2], obs_rs.at[2], (p, LAYERS - 1, a))

    def obs3_moved():
        others = forced_in.at[pl.ds(0, LAYERS - 1)]
        return remote(others, others, obs_ss.at[2], obs_rs.at[2], (1 - p, z, a))

    def late_copy():
        return remote(late_out, late_in, late_ss, late_rs, (p, z - 1, a))

    def send_layers(step, piece):
        start, stop = PIECES[piece]

        @pl.when(has_high)
        def _():
            layer_copy(step, 0, start, stop, piece).start()

        @pl.when(has_low)
        def _():
            layer_copy(step, 1, start, stop, piece).start()

    def take_layers(step, piece):
        start, stop = PIECES[piece]

        @pl.when(has_low)
        def _():
            layer_copy(step, 0, start, stop, piece).wait_recv()

        @pl.when(has_high)
        def _():
            layer_copy(step, 1, start, stop, piece).wait_recv()

    def send_rows(step):
        @pl.when(has_south)
        def _():
            row_copy(step, 0).start()

        @pl.when(has_north)
        def _():
            row_copy(step, 1).start()

    def take_rows(step):
        @pl.when(has_north)
        def _():
            row_copy(step, 0).wait_recv()

        @pl.when(has_south)
        def _():
            row_copy(step, 1).wait_recv()

    own_lane = iota((ROWS, LANES), 1) == (
        lax.rem(a, LANES // ROWS) * ROWS + iota((ROWS, LANES), 0)
    )

    def field_of(step, f):
        return scaled_f if step == 1 and f == FORCED else scaled[step].at[f]

    def fill_rows(step):
        for f in range(FIELDS):
            row_out[step, 0, f:f + 1, :] = field_of(step, f)[ROWS - 1:ROWS, :]
            row_out[step, 1, f:f + 1, :] = field_of(step, f)[0:1, :]

    def fill_edges(step):
        for f in range(FIELDS):
            for side, at in ((0, 0), (1, COLS - 1)):
                start = at // LANES * LANES
                block = field_of(step, f)[:, start:start + LANES]
                column = block[:, at - start:at - start + 1]
                wide = jnp.where(own_lane, jnp.broadcast_to(column, (ROWS, LANES)), 0.0)
                edge_out[step, side, f:f + 1, :] = jnp.sum(wide, axis=0, keepdims=True)

    def fill_base(step, source, target):
        rate = [[couple[e, c] for c in range(FIELDS)] for e in range(FIELDS)]
        for b in range(BLOCKS):
            cols = slice(b * LANES, (b + 1) * LANES)
            state = [source[e, :, cols] for e in range(FIELDS)]
            for c in range(FIELDS):
                total = state[c]
                for e in range(FIELDS):
                    total = total + rate[e][c] * state[e]
                target[c, :, cols] = total
        col_of = iota((ROWS, COLS), 1)
        row_of = iota((ROWS, COLS), 0)
        for f in range(FIELDS):
            s = field_of(step, f)[...]
            west = jnp.where(col_of == 0, 0.0, pltpu.roll(s, 1, 1))
            east = jnp.where(col_of == COLS - 1, 0.0, pltpu.roll(s, COLS - 1, 1))
            north = jnp.where(row_of == 0, 0.0, pltpu.roll(s, 1, 0))
            south = jnp.where(row_of == ROWS - 1, 0.0, pltpu.roll(s, ROWS - 1, 0))
            target[f] = target[f] + ((west + east) + (north + south) - 6.0 * s)

    def forward_edges(step):
        edges_moved(step).wait_recv()
        total = edge_in[step, 0] + edge_in[step, 1] + edge_in[step, 2] + edge_in[step, 3]
        edge_sum[step] = total
        for i in range(1, LINES):
            line_copy(step, i).start()
        edge_all[step, y] = total

    def add_ghost(step, target):
        lines_moved(step).wait_recv()
        half = LINES // 2
        for side in range(2):
            for h in range(2):
                total = edge_all[step, h * half, side]
                for i in range(1, half):
                    total = total + edge_all[step, h * half + i, side]
                edge_rows[side, 0:FIELDS, h * LANES:(h + 1) * LANES] = total
        for f in range(FIELDS):
            rows = [
                edge_rows[side, f:f + 1, :] * ghost_wt[side, point:point + 1, :]
                for side in range(2) for point in range(POINTS)
            ]
            top, rest = spread(high_hot[...], jnp.concatenate(rows, axis=1))
            spread_rows[f * HIGH:(f + 1) * HIGH] = top
            spread_rows[(FIELDS + f) * HIGH:(FIELDS + f + 1) * HIGH] = rest
        cells = dot_rows(spread_rows[...], low_hot[...])
        for f in range(FIELDS):
            for b in range(SPANS):
                at = f * HIGH + b * ROWS
                more = at + FIELDS * HIGH
                cols = slice(b * WIDE, (b + 1) * WIDE)
                target[f, :, cols] = target[f, :, cols] + (
                    cells[at:at + ROWS] + cells[more:more + ROWS]
                )

    for load in loads[:3]:
        load.wait()
    for f in range(FIELDS):
        scaled_a[f] = (diffus[f] * cond[...]) * adj[f]

    def count(flag):
        return jnp.where(flag, 1, 0)

    expected = (
        GROUP + LINES - 1 + GROUP - 1
        + count(has_low) + count(has_high) + count(has_north) + count(has_south) + count(inner)
    )
    pl.semaphore_wait(barrier, expected)

    for piece in range(len(PIECES)):
        send_layers(0, piece)
    fill_edges(0)
    for i in range(GROUP):
        edge_copy(0, i).start()
    fill_rows(0)
    send_rows(0)

    for load in loads[3:]:
        load.wait()
    owner_hot = jnp.where(iota((TILES, OBS), 0) == dest[...], 1.0, 0.0)
    earlier = jnp.where(iota((OBS, OBS), 1) < iota((OBS, OBS), 0), 1.0, 0.0).astype(BF16)
    before = dot_rows(owner_hot.astype(BF16), earlier)
    rank = jnp.sum(owner_hot * before, axis=0, keepdims=True)
    in_slot = rank == iota((SLOTS, OBS), 0, F32)
    number = cell[...]
    in_row = jnp.floor((number.astype(F32) + 0.5) * (1.0 / COLS)).astype(jnp.int32)
    column = number - in_row * COLS
    place = (
        (lax.shift_right_logical(column, 8) * ROWS + in_row) * WIDE + (column & (WIDE - 1))
    ).astype(F32)
    payload = []
    for kind in range(3):
        for point in range(POINTS):
            if kind < 2:
                row = misfit[kind:kind + 1, :] * obs_wt[point:point + 1, :]
            else:
                row = place[point:point + 1, :]
            payload.append(jnp.where(in_slot, jnp.broadcast_to(row, (SLOTS, OBS)), 0.0))
    packed = dot_rows(owner_hot, jnp.concatenate(payload, axis=0), lax.Precision.HIGHEST)
    width = SLOTS * POINTS
    own_half = iota((TILES, LANES), 1) // width == lax.rem(y, 2)
    for kind in range(3):
        part = packed[:, kind * width:(kind + 1) * width]
        outbox[:, kind, :] = jnp.where(own_half, jnp.concatenate([part, part], axis=1), 0.0)
    outbox[:, 3, :] = jnp.zeros((TILES, LANES), F32)
    for i in range(1, LINES):
        obs1_copy(i).start()
    line_in[y] = outbox[pl.ds(y * GROUP, GROUP)]

    forward_edges(0)

    for step in range(2):
        @pl.when(jnp.logical_not(has_low))
        def _():
            layer_in[step, 0] = jnp.zeros((FIELDS, ROWS, COLS), F32)

        @pl.when(jnp.logical_not(has_high))
        def _():
            layer_in[step, 1] = jnp.zeros((FIELDS, ROWS, COLS), F32)

        @pl.when(jnp.logical_not(has_north))
        def _():
            row_in[step, 0] = jnp.zeros((FIELDS, COLS), F32)

        @pl.when(jnp.logical_not(has_south))
        def _():
            row_in[step, 1] = jnp.zeros((FIELDS, COLS), F32)

    for side in range(2):
        for point in range(POINTS):
            at = (side * POINTS + point) * EDGE
            local = ghost_row[side, point:point + 1, :] - a * ROWS
            col = ghost_col[side, point:point + 1, :]
            inside = (local >= 0) & (local < ROWS)
            high = jnp.where(inside, lax.shift_right_logical(col, 8) * ROWS + local, -1)
            low = col & (WIDE - 1)
            high_hot[:, at:at + EDGE] = indicator(HIGH, high.astype(F32))
            low_hot[:, at:at + EDGE] = indicator(WIDE, low.astype(F32))

    obs1_moved().wait_recv()
    for i in range(GROUP):
        for pair in range(LINES // 2):
            pair_sum[i, pair] = line_in[2 * pair, i] + line_in[2 * pair + 1, i]
    for i in range(1, GROUP):
        obs2_copy(i).start()
    tile_in[q] = pair_sum[q]

    fill_base(0, adj, base)
    add_ghost(0, base)

    obs2_moved().wait_recv()

    @pl.when(inner)
    def _():
        obs3_copy().start()

    def with_halos(value, step, f, start, stop):
        size = stop - start
        row_of = iota((ROWS, size), 0)
        value = value + (layer_in[step, 0, f, :, start:stop] + layer_in[step, 1, f, :, start:stop])
        north = jnp.broadcast_to(row_in[step, 0, f:f + 1, start:stop], (ROWS, size))
        south = jnp.broadcast_to(row_in[step, 1, f:f + 1, start:stop], (ROWS, size))
        return value + jnp.where(row_of == 0, north, jnp.where(row_of == ROWS - 1, south, 0.0))

    take_rows(0)
    for piece, (start, stop) in enumerate(PIECES):
        take_layers(0, piece)
        for f in range(FIELDS):
            value = with_halos(base[f, :, start:stop], 0, f, start, stop)
            base[f, :, start:stop] = value
            scaled_b[f, :, start:stop] = (diffus[f] * cond[:, start:stop]) * value
        send_layers(1, piece)
    scaled_f[...] = scaled_b[FORCED]

    @pl.when(outer)
    def _():
        forced_in[LAYERS - 1] = tile_in[...]
        obs3_moved().wait_recv()
        forcing[...] = jnp.zeros((2 * HIGH, WIDE), F32)

        def one_layer(layer, carry):
            rows = [[], [], []]
            for i in range(GROUP):
                for pair in range(LINES // 2):
                    for kind in range(3):
                        rows[kind].append(forced_in[layer, i, pair, kind:kind + 1, :])
            early, late, places = [jnp.concatenate(r, axis=1) for r in rows]
            high = jnp.floor(places * (1.0 / WIDE))
            hot_high = indicator(HIGH, high)
            hot_low = indicator(WIDE, places - high * WIDE)
            top_a, rest_a = spread(hot_high, early)
            top_b, rest_b = spread(hot_high, late)
            cells = dot_rows(jnp.concatenate([top_a, top_b, rest_a, rest_b], axis=0), hot_low)
            forcing[...] = forcing[...] + (cells[:2 * HIGH] + cells[2 * HIGH:])
            return carry

        lax.fori_loop(0, LAYERS, one_layer, 0, unroll=2)
        for b in range(SPANS):
            cols = slice(b * WIDE, (b + 1) * WIDE)
            added = forcing[HIGH + b * ROWS:HIGH + (b + 1) * ROWS]
            share = (diffus[FORCED] * cond[:, cols]) * added
            base[FORCED, :, cols] = base[FORCED, :, cols] + added
            scaled_f[:, cols] = scaled_f[:, cols] + share
            late_out[:, cols] = share
        late_copy().start()

    fill_edges(1)
    for i in range(GROUP):
        edge_copy(1, i).start()
    fill_rows(1)
    send_rows(1)
    fill_base(1, base, out)
    forward_edges(1)
    add_ghost(1, out)

    @pl.when(outer)
    def _():
        for b in range(SPANS):
            cols = slice(b * WIDE, (b + 1) * WIDE)
            out[FORCED, :, cols] = out[FORCED, :, cols] + forcing[b * ROWS:(b + 1) * ROWS]

    take_rows(1)
    for piece, (start, stop) in enumerate(PIECES):
        take_layers(1, piece)
        for f in range(FIELDS):
            out[f, :, start:stop] = with_halos(out[f, :, start:stop], 1, f, start, stop)

    @pl.when(z == LAYERS - 2)
    def _():
        late_copy().wait_recv()
        out[FORCED] = out[FORCED] + late_in[...]

    for step in range(2):
        edges_moved(step).wait_send()
        lines_moved(step).wait_send()
        for way, flag in ((0, has_high), (1, has_low)):
            @pl.when(flag)
            def _():
                layer_copy(step, way).wait_send()

        for way, flag in ((0, has_south), (1, has_north)):
            @pl.when(flag)
            def _():
                row_copy(step, way).wait_send()

    obs1_moved().wait_send()
    obs2_moved().wait_send()

    @pl.when(inner)
    def _():
        obs3_copy().wait_send()

    @pl.when(outer)
    def _():
        late_copy().wait_send()


def steps(*operands):
    dma = pltpu.SemaphoreType.DMA
    state = (FIELDS, ROWS, COLS)
    terms = 2 * POINTS * EDGE
    pairs = LINES // 2
    inputs = [
        pltpu.SMEM(x.shape, x.dtype) if i in (2, 3) else pltpu.VMEM(x.shape, x.dtype)
        for i, x in enumerate(operands)
    ]
    return pl.pallas_call(
        kernel,
        out_shape=jax.ShapeDtypeStruct(state, F32),
        in_specs=[pl.BlockSpec(memory_space=pltpu.HBM)] * len(operands),
        out_specs=pl.BlockSpec(memory_space=pltpu.VMEM),
        scratch_shapes=inputs + [
            dma((len(operands),)),
            pltpu.VMEM(state, F32),
            pltpu.VMEM(state, F32),
            pltpu.VMEM(state[1:], F32),
            pltpu.VMEM(state, F32),
            pltpu.VMEM((2, 2) + state, F32),
            pltpu.VMEM((2, 2, FIELDS, COLS), F32),
            pltpu.VMEM((2, 2, FIELDS, COLS), F32),
            pltpu.VMEM((2, 2, FIELDS, LANES), F32),
            pltpu.VMEM((2, GROUP, 2, FIELDS, LANES), F32),
            pltpu.VMEM((2, 2, FIELDS, LANES), F32),
            pltpu.VMEM((2, LINES, 2, FIELDS, LANES), F32),
            pltpu.VMEM((2, 8, EDGE), F32),
            pltpu.VMEM((HIGH, terms), BF16),
            pltpu.VMEM((WIDE, terms), BF16),
            pltpu.VMEM((2 * FIELDS * HIGH, terms), BF16),
            pltpu.VMEM((TILES, 4, LANES), F32),
            pltpu.VMEM((LINES, GROUP, 4, LANES), F32),
            pltpu.VMEM((GROUP, pairs, 4, LANES), F32),
            pltpu.VMEM((GROUP, pairs, 4, LANES), F32),
            pltpu.VMEM((LAYERS, GROUP, pairs, 4, LANES), F32),
            pltpu.VMEM((2 * HIGH, WIDE), F32),
            pltpu.VMEM(state[1:], F32),
            pltpu.VMEM(state[1:], F32),
            dma((2, 2)), dma((2, 2, len(PIECES))),
            dma((2, 2)), dma((2, 2)),
            dma((2,)), dma((2,)),
            dma((2,)), dma((2,)),
            dma((3,)), dma((3,)),
            dma(()), dma(()),
        ],
        compiler_params=pltpu.CompilerParams(
            collective_id=0, has_side_effects=True, vmem_limit_bytes=60 << 20
        ),
        name="adjoint_steps",
    )(*operands)


def body(
    adj_final, cond, diffus, couple, ghost_row, ghost_col, ghost_wt, obs_dest, obs_cell, obs_wt,
    misfit,
):
    final = steps(
        adj_final.reshape(FIELDS, ROWS, COLS), cond[0, 0], diffus, couple, ghost_row, ghost_col,
        ghost_wt, obs_dest.reshape(1, OBS), obs_cell[0, 0], obs_wt[0, 0], misfit[0, 0],
    )
    return final[None, :, None]


def solution(mesh):
    placed = (
        P("panel", None, "rad", "ang", None),
        P("panel", "rad", "ang", None),
        P(),
        P(),
        P(),
        P(),
        P(),
        P("panel", "rad", "ang", None),
        P("panel", "rad", None, "ang"),
        P("panel", "rad", None, "ang"),
        P("panel", "rad", None, "ang"),
    )
    return jax.shard_map(
        body,
        mesh=mesh,
        in_specs=placed,
        out_specs=P("panel", None, "rad", "ang", None),
        check_vma=False,
    )
```

time: 51.3 us -> 37.9 us (0.74)
  the two profiles are of different devices: /device:TPU:448 before, /device:TPU:1 now
where the time goes in v2:
time: 37.9 us; the launch traced here: 37.8 us
  Pallas kernels  36 us (95%)
  local copies, waits for them, and re-layouts  1.73 us (5%)
    pallas_call x1, Pallas kernels, steps(): pl.pallas_call(kernel, out_shape=jax.ShapeDtypeStruct(state, F32), in_spe...  36 us
    unnamed x1, local copies, waits for them, and re-layouts  1.73 us

profile of v2, /device:TPU:1, one launch (start us, length us, event | category | flops | bytes accessed | tf_op | source)
XLA Modules:
  0.0 37.8 jit_solution(17525262667450397167)
XLA Ops:
  0.0 36.0 %adjoint_steps.1 = f32[7,8,1536]{2,1,0:T(8,128)} custom-call(f32[7,8,1536]{2,1,0:T(8,128)} %bitcast.10, f32[8,1536]{1,0:T(8,128)} %bitcast.11, f32[7]{0:T(128)} %diffus_hbm.1, f32[7,7]{1,0:T(8,128)} %couple_hbm.1, s32[2,4,256]{2,1,0:T(4,128)} %ghost_row_hbm.1, s32[2,4,256]{2,1,0:T(4,128)} %ghost_col_hbm.1, f32[2,4,256]{2,1,0:T(4,128)} %ghost_wt_hbm.1, ...), custom_call_target="tpu_custom_call" | custom-call | tf_op jit(solution)/shard_map/adjoint_steps/pallas_call | solution.py:525
  36.0 1.7 %copy.14 = f32[1,7,1,8,1536]{4,3,2,1,0:T(8,128)} copy(f32[1,7,1,8,1536]{4,3,2,1,0:T(8,128)} %bitcast.9) | data formatting | bytes 688128

commit v3 on v2

--- a/solution.py
+++ b/solution.py
@@ -16,13 +16,15 @@
 HIGH = ROWS * SPANS
 LAYERS, TILES, GROUP = 8, 32, 4
 LINES = TILES // GROUP
+HALF = LAYERS // 2
 SLOTS = 16
 POINTS = 4
 OBS = 256
 EDGE = TILES * ROWS
 FORCED = 3
 
-PIECES = ((0, 512), (512, 1024), (1024, 1536))
+PIECES = ((0, 128), (1408, 1536), (128, 1408))
+EDGE_PIECES = 2
 
 
 def iota(shape, dim, dtype=jnp.int32):
@@ -57,11 +59,11 @@
     out,
     adj, cond, diffus, couple, ghost_row, ghost_col, ghost_wt, dest, cell, obs_wt, misfit, load_s,
     scaled_a, scaled_b, scaled_f, base, layer_in, row_out, row_in,
-    edge_out, edge_in, edge_sum, edge_all, edge_rows,
+    edge_out, edge_all, edge_rows,
     high_hot, low_hot, spread_rows,
     outbox, line_in, pair_sum, tile_in, forced_in, forcing, late_out, late_in,
     layer_ss, layer_rs, row_ss, row_rs,
-    edge_ss, edge_rs, line_ss, line_rs, obs_ss, obs_rs, late_ss, late_rs,
+    edge_ss, edge_rs, obs_ss, obs_rs, late_ss, late_rs, open_s,
 ):
     loads = [
         pltpu.make_async_copy(source, target, load_s.at[i])
@@ -93,6 +95,12 @@
     def greet(panel, layer, tile):
         pl.semaphore_signal(barrier, inc=1, device_id=(panel, layer, tile), device_id_type=MESH)
 
+    order = sorted(range(TILES), key=lambda i: -min(i, TILES - i))
+    for i in order:
+        greet(1 - p, z, lax.rem(a + i, TILES))
+    for i in sorted(range(1, LINES), key=lambda i: -min(i, LINES - i)):
+        greet(p, z, along_line(i) * GROUP + q)
+
     @pl.when(has_low)
     def _():
         greet(p, z - 1, a)
@@ -109,17 +117,12 @@
     def _():
         greet(p, z, a + 1)
 
-    for i in range(GROUP):
-        greet(1 - p, z, y * GROUP + i)
-    for i in range(1, LINES):
-        greet(p, z, along_line(i) * GROUP + q)
     for i in range(1, GROUP):
         greet(p, z, y * GROUP + beside(i))
 
-    @pl.when(outer)
-    def _():
-        for i in range(LAYERS - 1):
-            greet(p, i, a)
+    @pl.when(inner)
+    def _():
+        greet(p, LAYERS - 1, a)
 
     for load in loads[3:]:
         load.start()
@@ -145,23 +148,13 @@
 
     def edge_copy(step, i):
         return remote(
-            edge_out.at[step], edge_in.at[step, q], edge_ss.at[step], edge_rs.at[step],
-            (1 - p, z, y * GROUP + i),
+            edge_out.at[step], edge_all.at[step, pl.ds(a, 1), :], edge_ss.at[step], edge_rs.at[step],
+            (1 - p, z, lax.rem(a + i, TILES)),
         )
 
     def edges_moved(step):
-        everything = edge_in.at[step]
+        everything = edge_all.at[step]
         return remote(everything, everything, edge_ss.at[step], edge_rs.at[step], (1 - p, z, a))
-
-    def line_copy(step, i):
-        return remote(
-            edge_sum.at[step], edge_all.at[step, y], line_ss.at[step], line_rs.at[step],
-            (p, z, along_line(i) * GROUP + q),
-        )
-
-    def lines_moved(step):
-        others = edge_all.at[step, pl.ds(0, LINES - 1)]
-        return remote(others, others, line_ss.at[step], line_rs.at[step], (1 - p, z, a))
 
     def obs1_copy(i):
         target = along_line(i)
@@ -186,11 +179,15 @@
         return remote(others, others, obs_ss.at[1], obs_rs.at[1], (1 - p, z, a))
 
     def obs3_copy():
-        return remote(tile_in, forced_in.at[z], obs_ss.at[2], obs_rs.at[2], (p, LAYERS - 1, a))
-
-    def obs3_moved():
-        others = forced_in.at[pl.ds(0, LAYERS - 1)]
-        return remote(others, others, obs_ss.at[2], obs_rs.at[2], (1 - p, z, a))
+        return remote(
+            tile_in, forced_in.at[z], obs_ss.at[2], obs_rs.at[2 + z // HALF], (p, LAYERS - 1, a)
+        )
+
+    def obs3_moved(start, count):
+        others = forced_in.at[pl.ds(start, count)]
+        return remote(
+            others, others, obs_ss.at[2], obs_rs.at[2 + start // HALF], (1 - p, z, a)
+        )
 
     def late_copy():
         return remote(late_out, late_in, late_ss, late_rs, (p, z - 1, a))
@@ -235,26 +232,38 @@
         def _():
             row_copy(step, 1).wait_recv()
 
-    own_lane = iota((ROWS, LANES), 1) == (
-        lax.rem(a, LANES // ROWS) * ROWS + iota((ROWS, LANES), 0)
-    )
-
     def field_of(step, f):
         return scaled_f if step == 1 and f == FORCED else scaled[step].at[f]
 
+    runs = LANES // ROWS
+    lane_of = iota((ROWS, LANES), 1)
+    own_run = jnp.where(
+        lax.rem(lane_of, ROWS) == iota((ROWS, LANES), 0),
+        lax.rem(lane_of // ROWS - lax.rem(a, runs) + runs, runs), -1,
+    )
+    sent_run = lax.rem(iota((runs, LANES), 1) // ROWS - iota((runs, LANES), 0) + runs, runs)
+
     def fill_rows(step):
         for f in range(FIELDS):
             row_out[step, 0, f:f + 1, :] = field_of(step, f)[ROWS - 1:ROWS, :]
             row_out[step, 1, f:f + 1, :] = field_of(step, f)[0:1, :]
 
     def fill_edges(step):
+        wide = jnp.zeros((ROWS, LANES), F32)
         for f in range(FIELDS):
             for side, at in ((0, 0), (1, COLS - 1)):
                 start = at // LANES * LANES
                 block = field_of(step, f)[:, start:start + LANES]
                 column = block[:, at - start:at - start + 1]
-                wide = jnp.where(own_lane, jnp.broadcast_to(column, (ROWS, LANES)), 0.0)
-                edge_out[step, side, f:f + 1, :] = jnp.sum(wide, axis=0, keepdims=True)
+                wide = jnp.where(
+                    own_run == 2 * f + side, jnp.broadcast_to(column, (ROWS, LANES)), wide
+                )
+        edge_out[step] = jnp.sum(wide, axis=0, keepdims=True)
+
+    def send_edges(step):
+        fill_edges(step)
+        for i in order:
+            edge_copy(step, i).start()
 
     def fill_base(step, source, target):
         rate = [[couple[e, c] for c in range(FIELDS)] for e in range(FIELDS)]
@@ -276,23 +285,19 @@
             south = jnp.where(row_of == ROWS - 1, 0.0, pltpu.roll(s, ROWS - 1, 0))
             target[f] = target[f] + ((west + east) + (north + south) - 6.0 * s)
 
-    def forward_edges(step):
+    def add_ghost(step, target):
         edges_moved(step).wait_recv()
-        total = edge_in[step, 0] + edge_in[step, 1] + edge_in[step, 2] + edge_in[step, 3]
-        edge_sum[step] = total
-        for i in range(1, LINES):
-            line_copy(step, i).start()
-        edge_all[step, y] = total
-
-    def add_ghost(step, target):
-        lines_moved(step).wait_recv()
-        half = LINES // 2
-        for side in range(2):
-            for h in range(2):
-                total = edge_all[step, h * half, side]
-                for i in range(1, half):
-                    total = total + edge_all[step, h * half + i, side]
-                edge_rows[side, 0:FIELDS, h * LANES:(h + 1) * LANES] = total
+        for f in range(FIELDS):
+            for side in range(2):
+                run = 2 * f + side
+                for h in range(2):
+                    part = jnp.where(
+                        sent_run == run, edge_all[step, h * runs:(h + 1) * runs, :], 0.0
+                    )
+                    line = jnp.sum(part, axis=0, keepdims=True)
+                    if run:
+                        line = pltpu.roll(line, LANES - ROWS * run, 1)
+                    edge_rows[side, f:f + 1, h * LANES:(h + 1) * LANES] = line
         for f in range(FIELDS):
             rows = [
                 edge_rows[side, f:f + 1, :] * ghost_wt[side, point:point + 1, :]
@@ -316,22 +321,8 @@
     for f in range(FIELDS):
         scaled_a[f] = (diffus[f] * cond[...]) * adj[f]
 
-    def count(flag):
-        return jnp.where(flag, 1, 0)
-
-    expected = (
-        GROUP + LINES - 1 + GROUP - 1
-        + count(has_low) + count(has_high) + count(has_north) + count(has_south) + count(inner)
-    )
-    pl.semaphore_wait(barrier, expected)
-
-    for piece in range(len(PIECES)):
-        send_layers(0, piece)
     fill_edges(0)
-    for i in range(GROUP):
-        edge_copy(0, i).start()
     fill_rows(0)
-    send_rows(0)
 
     for load in loads[3:]:
         load.wait()
@@ -361,29 +352,6 @@
         part = packed[:, kind * width:(kind + 1) * width]
         outbox[:, kind, :] = jnp.where(own_half, jnp.concatenate([part, part], axis=1), 0.0)
     outbox[:, 3, :] = jnp.zeros((TILES, LANES), F32)
-    for i in range(1, LINES):
-        obs1_copy(i).start()
-    line_in[y] = outbox[pl.ds(y * GROUP, GROUP)]
-
-    forward_edges(0)
-
-    for step in range(2):
-        @pl.when(jnp.logical_not(has_low))
-        def _():
-            layer_in[step, 0] = jnp.zeros((FIELDS, ROWS, COLS), F32)
-
-        @pl.when(jnp.logical_not(has_high))
-        def _():
-            layer_in[step, 1] = jnp.zeros((FIELDS, ROWS, COLS), F32)
-
-        @pl.when(jnp.logical_not(has_north))
-        def _():
-            row_in[step, 0] = jnp.zeros((FIELDS, COLS), F32)
-
-        @pl.when(jnp.logical_not(has_south))
-        def _():
-            row_in[step, 1] = jnp.zeros((FIELDS, COLS), F32)
-
     for side in range(2):
         for point in range(POINTS):
             at = (side * POINTS + point) * EDGE
@@ -395,6 +363,31 @@
             high_hot[:, at:at + EDGE] = indicator(HIGH, high.astype(F32))
             low_hot[:, at:at + EDGE] = indicator(WIDE, low.astype(F32))
 
+    def count(flag):
+        return jnp.where(flag, 1, 0)
+
+    expected = (
+        TILES + LINES - 1 + GROUP - 1
+        + count(has_low) + count(has_high) + count(has_north) + count(has_south)
+        + jnp.where(outer, LAYERS - 1, 0)
+    )
+    pl.semaphore_wait(barrier, expected)
+
+    @pl.when(outer)
+    def _():
+        for i in range(LAYERS - 1):
+            pl.semaphore_signal(open_s, inc=1, device_id=(p, i, a), device_id_type=MESH)
+
+    for i in range(1, LINES):
+        obs1_copy(i).start()
+    line_in[y] = outbox[pl.ds(y * GROUP, GROUP)]
+
+    for i in order:
+        edge_copy(0, i).start()
+    for piece in range(EDGE_PIECES + 1):
+        send_layers(0, piece)
+    send_rows(0)
+
     obs1_moved().wait_recv()
     for i in range(GROUP):
         for pair in range(LINES // 2):
@@ -403,14 +396,54 @@
         obs2_copy(i).start()
     tile_in[q] = pair_sum[q]
 
+    for step in range(2):
+        @pl.when(jnp.logical_not(has_low))
+        def _():
+            layer_in[step, 0] = jnp.zeros((FIELDS, ROWS, COLS), F32)
+
+        @pl.when(jnp.logical_not(has_high))
+        def _():
+            layer_in[step, 1] = jnp.zeros((FIELDS, ROWS, COLS), F32)
+
+        @pl.when(jnp.logical_not(has_north))
+        def _():
+            row_in[step, 0] = jnp.zeros((FIELDS, COLS), F32)
+
+        @pl.when(jnp.logical_not(has_south))
+        def _():
+            row_in[step, 1] = jnp.zeros((FIELDS, COLS), F32)
+
     fill_base(0, adj, base)
+    obs2_moved().wait_recv()
+
+    @pl.when(inner)
+    def _():
+        pl.semaphore_wait(open_s, 1)
+        obs3_copy().start()
+
     add_ghost(0, base)
 
-    obs2_moved().wait_recv()
-
-    @pl.when(inner)
-    def _():
-        obs3_copy().start()
+    def one_layer(layer, carry):
+        rows = [[], [], []]
+        for i in range(GROUP):
+            for pair in range(LINES // 2):
+                for kind in range(3):
+                    rows[kind].append(forced_in[layer, i, pair, kind:kind + 1, :])
+        early, late, places = [jnp.concatenate(r, axis=1) for r in rows]
+        high = jnp.floor(places * (1.0 / WIDE))
+        hot_high = indicator(HIGH, high)
+        hot_low = indicator(WIDE, places - high * WIDE)
+        top_a, rest_a = spread(hot_high, early)
+        top_b, rest_b = spread(hot_high, late)
+        cells = dot_rows(jnp.concatenate([top_a, top_b, rest_a, rest_b], axis=0), hot_low)
+        forcing[...] = forcing[...] + (cells[:2 * HIGH] + cells[2 * HIGH:])
+        return carry
+
+    @pl.when(outer)
+    def _():
+        forcing[...] = jnp.zeros((2 * HIGH, WIDE), F32)
+        obs3_moved(0, HALF).wait_recv()
+        lax.fori_loop(0, HALF, one_layer, 0, unroll=2)
 
     def with_halos(value, step, f, start, stop):
         size = stop - start
@@ -428,31 +461,20 @@
             base[f, :, start:stop] = value
             scaled_b[f, :, start:stop] = (diffus[f] * cond[:, start:stop]) * value
         send_layers(1, piece)
+        if piece == EDGE_PIECES - 1:
+            scaled_f[:, :LANES] = scaled_b[FORCED, :, :LANES]
+            scaled_f[:, COLS - LANES:] = scaled_b[FORCED, :, COLS - LANES:]
+
+            @pl.when(inner)
+            def _():
+                send_edges(1)
     scaled_f[...] = scaled_b[FORCED]
 
     @pl.when(outer)
     def _():
         forced_in[LAYERS - 1] = tile_in[...]
-        obs3_moved().wait_recv()
-        forcing[...] = jnp.zeros((2 * HIGH, WIDE), F32)
-
-        def one_layer(layer, carry):
-            rows = [[], [], []]
-            for i in range(GROUP):
-                for pair in range(LINES // 2):
-                    for kind in range(3):
-                        rows[kind].append(forced_in[layer, i, pair, kind:kind + 1, :])
-            early, late, places = [jnp.concatenate(r, axis=1) for r in rows]
-            high = jnp.floor(places * (1.0 / WIDE))
-            hot_high = indicator(HIGH, high)
-            hot_low = indicator(WIDE, places - high * WIDE)
-            top_a, rest_a = spread(hot_high, early)
-            top_b, rest_b = spread(hot_high, late)
-            cells = dot_rows(jnp.concatenate([top_a, top_b, rest_a, rest_b], axis=0), hot_low)
-            forcing[...] = forcing[...] + (cells[:2 * HIGH] + cells[2 * HIGH:])
-            return carry
-
-        lax.fori_loop(0, LAYERS, one_layer, 0, unroll=2)
+        obs3_moved(HALF, HALF - 1).wait_recv()
+        lax.fori_loop(HALF, LAYERS, one_layer, 0, unroll=2)
         for b in range(SPANS):
             cols = slice(b * WIDE, (b + 1) * WIDE)
             added = forcing[HIGH + b * ROWS:HIGH + (b + 1) * ROWS]
@@ -460,15 +482,14 @@
             base[FORCED, :, cols] = base[FORCED, :, cols] + added
             scaled_f[:, cols] = scaled_f[:, cols] + share
             late_out[:, cols] = share
+        send_edges(1)
         late_copy().start()
 
-    fill_edges(1)
-    for i in range(GROUP):
-        edge_copy(1, i).start()
     fill_rows(1)
     send_rows(1)
+
     fill_base(1, base, out)
-    forward_edges(1)
+
     add_ghost(1, out)
 
     @pl.when(outer)
@@ -490,7 +511,6 @@
 
     for step in range(2):
         edges_moved(step).wait_send()
-        lines_moved(step).wait_send()
         for way, flag in ((0, has_high), (1, has_low)):
             @pl.when(flag)
             def _():
@@ -536,10 +556,8 @@
             pltpu.VMEM((2, 2) + state, F32),
             pltpu.VMEM((2, 2, FIELDS, COLS), F32),
             pltpu.VMEM((2, 2, FIELDS, COLS), F32),
-            pltpu.VMEM((2, 2, FIELDS, LANES), F32),
-            pltpu.VMEM((2, GROUP, 2, FIELDS, LANES), F32),
-            pltpu.VMEM((2, 2, FIELDS, LANES), F32),
-            pltpu.VMEM((2, LINES, 2, FIELDS, LANES), F32),
+            pltpu.VMEM((2, 1, LANES), F32),
+            pltpu.VMEM((2, TILES, LANES), F32),
             pltpu.VMEM((2, 8, EDGE), F32),
             pltpu.VMEM((HIGH, terms), BF16),
             pltpu.VMEM((WIDE, terms), BF16),
@@ -555,9 +573,8 @@
             dma((2, 2)), dma((2, 2, len(PIECES))),
             dma((2, 2)), dma((2, 2)),
             dma((2,)), dma((2,)),
-            dma((2,)), dma((2,)),
-            dma((3,)), dma((3,)),
-            dma(()), dma(()),
+            dma((3,)), dma((4,)),
+            dma(()), dma(()), pltpu.SemaphoreType.REGULAR,
         ],
         compiler_params=pltpu.CompilerParams(
             collective_id=0, has_side_effects=True, vmem_limit_bytes=60 << 20

time: 37.9 us -> 34.1 us (0.90)
  Pallas kernels: 36 us -> 32.1 us
    pallas_call x1, Pallas kernels: 36 us -> 32.1 us  [steps(): pl.pallas_call(kernel, out_shape=jax.ShapeDtypeStruct(state, F32), in_spe...]
where the time goes in v3:
time: 34.1 us; the launch traced here: 33.9 us
  Pallas kernels  32.1 us (94%)
  local copies, waits for them, and re-layouts  1.73 us (5%)
    pallas_call x1, Pallas kernels, steps(): pl.pallas_call(kernel, out_shape=jax.ShapeDtypeStruct(state, F32), in_spe...  32.1 us
    unnamed x1, local copies, waits for them, and re-layouts  1.73 us

profile of v3, /device:TPU:1, one launch (start us, length us, event | category | flops | bytes accessed | tf_op | source)
XLA Modules:
  0.0 33.9 jit_solution(14092481116141496982)
XLA Ops:
  0.0 32.1 %adjoint_steps.1 = f32[7,8,1536]{2,1,0:T(8,128)} custom-call(f32[7,8,1536]{2,1,0:T(8,128)} %bitcast.10, f32[8,1536]{1,0:T(8,128)} %bitcast.11, f32[7]{0:T(128)} %diffus_hbm.1, f32[7,7]{1,0:T(8,128)} %couple_hbm.1, s32[2,4,256]{2,1,0:T(4,128)} %ghost_row_hbm.1, s32[2,4,256]{2,1,0:T(4,128)} %ghost_col_hbm.1, f32[2,4,256]{2,1,0:T(4,128)} %ghost_wt_hbm.1, ...), custom_call_target="tpu_custom_call" | custom-call | tf_op jit(solution)/shard_map/adjoint_steps/pallas_call | solution.py:545
  32.1 1.7 %copy.14 = f32[1,7,1,8,1536]{4,3,2,1,0:T(8,128)} copy(f32[1,7,1,8,1536]{4,3,2,1,0:T(8,128)} %bitcast.9) | data formatting | bytes 688128

commit v4 on v3

--- a/solution.py
+++ b/solution.py
@@ -23,7 +23,7 @@
 EDGE = TILES * ROWS
 FORCED = 3
 
-PIECES = ((0, 128), (1408, 1536), (128, 1408))
+PIECES = ((0, 128), (1408, 1536), (128, 768), (768, 1408))
 EDGE_PIECES = 2
 
 
@@ -384,7 +384,7 @@
 
     for i in order:
         edge_copy(0, i).start()
-    for piece in range(EDGE_PIECES + 1):
+    for piece in range(len(PIECES)):
         send_layers(0, piece)
     send_rows(0)
 
@@ -416,10 +416,13 @@
     fill_base(0, adj, base)
     obs2_moved().wait_recv()
 
-    @pl.when(inner)
-    def _():
-        pl.semaphore_wait(open_s, 1)
-        obs3_copy().start()
+    def send_third(flag):
+        @pl.when(flag)
+        def _():
+            pl.semaphore_wait(open_s, 1)
+            obs3_copy().start()
+
+    send_third(inner & (z >= 2))
 
     add_ghost(0, base)
 
@@ -468,6 +471,8 @@
             @pl.when(inner)
             def _():
                 send_edges(1)
+
+            send_third(z < 2)
     scaled_f[...] = scaled_b[FORCED]
 
     @pl.when(outer)
@@ -544,7 +549,7 @@
     ]
     return pl.pallas_call(
         kernel,
-        out_shape=jax.ShapeDtypeStruct(state, F32),
+        out_shape=pltpu.VMEM(state, F32),
         in_specs=[pl.BlockSpec(memory_space=pltpu.HBM)] * len(operands),
         out_specs=pl.BlockSpec(memory_space=pltpu.VMEM),
         scratch_shapes=inputs + [
@@ -577,7 +582,7 @@
             dma(()), dma(()), pltpu.SemaphoreType.REGULAR,
         ],
         compiler_params=pltpu.CompilerParams(
-            collective_id=0, has_side_effects=True, vmem_limit_bytes=60 << 20
+            collective_id=0, has_side_effects=True, vmem_limit_bytes=61440 << 10
         ),
         name="adjoint_steps",
     )(*operands)

time: 34.1 us -> 31.5 us (0.924)
  Pallas kernels: 32.1 us -> 30.6 us
  local copies, waits for them, and re-layouts: 1.73 us -> 0.73 us
    pallas_call x1, Pallas kernels: 32.1 us -> 30.6 us  [steps(): pl.pallas_call(kernel, out_shape=pltpu.VMEM(state, F32), in_specs=[pl.Blo...]
    unnamed x1, local copies, waits for them, and re-layouts: 1.73 us -> 0.73 us
where the time goes in v4:
time: 31.5 us; the launch traced here: 31.3 us
  Pallas kernels  30.6 us (97%)
  local copies, waits for them, and re-layouts  0.73 us (2%)
    pallas_call x1, Pallas kernels, steps(): pl.pallas_call(kernel, out_shape=pltpu.VMEM(state, F32), in_specs=[pl.Blo...  30.6 us
    unnamed x1, local copies, waits for them, and re-layouts  0.73 us

profile of v4, /device:TPU:1, one launch (start us, length us, event | category | flops | bytes accessed | tf_op | source)
XLA Modules:
  0.0 31.3 jit_solution(15352700329906233897)
XLA Ops:
  0.0 30.6 %adjoint_steps.1 = f32[7,8,1536]{2,1,0:T(8,128)S(1)} custom-call(f32[7,8,1536]{2,1,0:T(8,128)} %bitcast.10, f32[8,1536]{1,0:T(8,128)} %bitcast.11, f32[7]{0:T(128)} %diffus_hbm.1, f32[7,7]{1,0:T(8,128)} %couple_hbm.1, s32[2,4,256]{2,1,0:T(4,128)} %ghost_row_hbm.1, s32[2,4,256]{2,1,0:T(4,128)} %ghost_col_hbm.1, f32[2,4,256]{2,1,0:T(4,128)} %ghost_wt_hbm.1, ...), custom_call_target="tpu_custom_call" | custom-call | tf_op jit(solution)/shard_map/adjoint_steps/pallas_call | solution.py:550
  30.6 0.7 %copy.14 = f32[1,7,1,8,1536]{4,3,2,1,0:T(8,128)} copy(f32[1,7,1,8,1536]{4,3,2,1,0:T(8,128)S(1)} %bitcast.9) | data formatting | bytes 688128

commit v5 on v4

--- a/solution.py
+++ b/solution.py
@@ -61,7 +61,7 @@
     scaled_a, scaled_b, scaled_f, base, layer_in, row_out, row_in,
     edge_out, edge_all, edge_rows,
     high_hot, low_hot, spread_rows,
-    outbox, line_in, pair_sum, tile_in, forced_in, forcing, late_out, late_in,
+    outbox, line_in, tile_in, forced_in, forcing, late_out, late_in,
     layer_ss, layer_rs, row_ss, row_rs,
     edge_ss, edge_rs, obs_ss, obs_rs, late_ss, late_rs, open_s,
 ):
@@ -84,12 +84,6 @@
     inner = z < LAYERS - 1
     scaled = (scaled_a, scaled_b)
 
-    def along_line(step):
-        return lax.rem(y + step, LINES)
-
-    def beside(step):
-        return lax.rem(q + step, GROUP)
-
     barrier = pltpu.get_barrier_semaphore()
 
     def greet(panel, layer, tile):
@@ -98,8 +92,8 @@
     order = sorted(range(TILES), key=lambda i: -min(i, TILES - i))
     for i in order:
         greet(1 - p, z, lax.rem(a + i, TILES))
-    for i in sorted(range(1, LINES), key=lambda i: -min(i, LINES - i)):
-        greet(p, z, along_line(i) * GROUP + q)
+        if i:
+            greet(p, z, lax.rem(a + i, TILES))
 
     @pl.when(has_low)
     def _():
@@ -117,8 +111,6 @@
     def _():
         greet(p, z, a + 1)
 
-    for i in range(1, GROUP):
-        greet(p, z, y * GROUP + beside(i))
 
     @pl.when(inner)
     def _():
@@ -157,26 +149,14 @@
         return remote(everything, everything, edge_ss.at[step], edge_rs.at[step], (1 - p, z, a))
 
     def obs1_copy(i):
-        target = along_line(i)
+        target = lax.rem(a + i, TILES)
         return remote(
-            outbox.at[pl.ds(target * GROUP, GROUP)], line_in.at[y], obs_ss.at[0], obs_rs.at[0],
-            (p, z, target * GROUP + q),
+            outbox.at[target], line_in.at[a], obs_ss.at[0], obs_rs.at[0], (p, z, target)
         )
 
     def obs1_moved():
-        others = line_in.at[pl.ds(0, LINES - 1)]
+        others = line_in.at[pl.ds(0, TILES - 1)]
         return remote(others, others, obs_ss.at[0], obs_rs.at[0], (1 - p, z, a))
-
-    def obs2_copy(i):
-        target = beside(i)
-        return remote(
-            pair_sum.at[target], tile_in.at[q], obs_ss.at[1], obs_rs.at[1],
-            (p, z, y * GROUP + target),
-        )
-
-    def obs2_moved():
-        others = tile_in.at[pl.ds(0, GROUP - 1)]
-        return remote(others, others, obs_ss.at[1], obs_rs.at[1], (1 - p, z, a))
 
     def obs3_copy():
         return remote(
@@ -367,7 +347,7 @@
         return jnp.where(flag, 1, 0)
 
     expected = (
-        TILES + LINES - 1 + GROUP - 1
+        TILES + TILES - 1
         + count(has_low) + count(has_high) + count(has_north) + count(has_south)
         + jnp.where(outer, LAYERS - 1, 0)
     )
@@ -378,9 +358,10 @@
         for i in range(LAYERS - 1):
             pl.semaphore_signal(open_s, inc=1, device_id=(p, i, a), device_id_type=MESH)
 
-    for i in range(1, LINES):
-        obs1_copy(i).start()
-    line_in[y] = outbox[pl.ds(y * GROUP, GROUP)]
+    for i in order:
+        if i:
+            obs1_copy(i).start()
+    line_in[a] = outbox[a]
 
     for i in order:
         edge_copy(0, i).start()
@@ -388,33 +369,29 @@
         send_layers(0, piece)
     send_rows(0)
 
+    for step in range(2):
+        @pl.when(jnp.logical_not(has_low))
+        def _():
+            layer_in[step, 0] = jnp.zeros((FIELDS, ROWS, COLS), F32)
+
+        @pl.when(jnp.logical_not(has_high))
+        def _():
+            layer_in[step, 1] = jnp.zeros((FIELDS, ROWS, COLS), F32)
+
+        @pl.when(jnp.logical_not(has_north))
+        def _():
+            row_in[step, 0] = jnp.zeros((FIELDS, COLS), F32)
+
+        @pl.when(jnp.logical_not(has_south))
+        def _():
+            row_in[step, 1] = jnp.zeros((FIELDS, COLS), F32)
+
+    fill_base(0, adj, base)
     obs1_moved().wait_recv()
     for i in range(GROUP):
         for pair in range(LINES // 2):
-            pair_sum[i, pair] = line_in[2 * pair, i] + line_in[2 * pair + 1, i]
-    for i in range(1, GROUP):
-        obs2_copy(i).start()
-    tile_in[q] = pair_sum[q]
-
-    for step in range(2):
-        @pl.when(jnp.logical_not(has_low))
-        def _():
-            layer_in[step, 0] = jnp.zeros((FIELDS, ROWS, COLS), F32)
-
-        @pl.when(jnp.logical_not(has_high))
-        def _():
-            layer_in[step, 1] = jnp.zeros((FIELDS, ROWS, COLS), F32)
-
-        @pl.when(jnp.logical_not(has_north))
-        def _():
-            row_in[step, 0] = jnp.zeros((FIELDS, COLS), F32)
-
-        @pl.when(jnp.logical_not(has_south))
-        def _():
-            row_in[step, 1] = jnp.zeros((FIELDS, COLS), F32)
-
-    fill_base(0, adj, base)
-    obs2_moved().wait_recv()
+            tile = 2 * pair * GROUP + i
+            tile_in[i, pair] = line_in[tile] + line_in[tile + GROUP]
 
     def send_third(flag):
         @pl.when(flag)
@@ -442,12 +419,6 @@
         forcing[...] = forcing[...] + (cells[:2 * HIGH] + cells[2 * HIGH:])
         return carry
 
-    @pl.when(outer)
-    def _():
-        forcing[...] = jnp.zeros((2 * HIGH, WIDE), F32)
-        obs3_moved(0, HALF).wait_recv()
-        lax.fori_loop(0, HALF, one_layer, 0, unroll=2)
-
     def with_halos(value, step, f, start, stop):
         size = stop - start
         row_of = iota((ROWS, size), 0)
@@ -474,6 +445,12 @@
 
             send_third(z < 2)
     scaled_f[...] = scaled_b[FORCED]
+
+    @pl.when(outer)
+    def _():
+        forcing[...] = jnp.zeros((2 * HIGH, WIDE), F32)
+        obs3_moved(0, HALF).wait_recv()
+        lax.fori_loop(0, HALF, one_layer, 0, unroll=2)
 
     @pl.when(outer)
     def _():
@@ -527,7 +504,6 @@
                 row_copy(step, way).wait_send()
 
     obs1_moved().wait_send()
-    obs2_moved().wait_send()
 
     @pl.when(inner)
     def _():
@@ -568,8 +544,7 @@
             pltpu.VMEM((WIDE, terms), BF16),
             pltpu.VMEM((2 * FIELDS * HIGH, terms), BF16),
             pltpu.VMEM((TILES, 4, LANES), F32),
-            pltpu.VMEM((LINES, GROUP, 4, LANES), F32),
-            pltpu.VMEM((GROUP, pairs, 4, LANES), F32),
+            pltpu.VMEM((TILES, 4, LANES), F32),
             pltpu.VMEM((GROUP, pairs, 4, LANES), F32),
             pltpu.VMEM((LAYERS, GROUP, pairs, 4, LANES), F32),
             pltpu.VMEM((2 * HIGH, WIDE), F32),

time: 31.5 us -> 31.7 us (level)
  no operation moved by 1% of the time
where the time goes in v5:
time: 31.7 us; the launch traced here: 31.5 us
  Pallas kernels  30.8 us (97%)
  local copies, waits for them, and re-layouts  0.73 us (2%)
    pallas_call x1, Pallas kernels, steps(): pl.pallas_call(kernel, out_shape=pltpu.VMEM(state, F32), in_specs=[pl.Blo...  30.8 us
    unnamed x1, local copies, waits for them, and re-layouts  0.73 us

profile of v5, /device:TPU:1, one launch (start us, length us, event | category | flops | bytes accessed | tf_op | source)
XLA Modules:
  0.0 31.5 jit_solution(15181294181877639559)
XLA Ops:
  0.0 30.8 %adjoint_steps.1 = f32[7,8,1536]{2,1,0:T(8,128)S(1)} custom-call(f32[7,8,1536]{2,1,0:T(8,128)} %bitcast.10, f32[8,1536]{1,0:T(8,128)} %bitcast.11, f32[7]{0:T(128)} %diffus_hbm.1, f32[7,7]{1,0:T(8,128)} %couple_hbm.1, s32[2,4,256]{2,1,0:T(4,128)} %ghost_row_hbm.1, s32[2,4,256]{2,1,0:T(4,128)} %ghost_col_hbm.1, f32[2,4,256]{2,1,0:T(4,128)} %ghost_wt_hbm.1, ...), custom_call_target="tpu_custom_call" | custom-call | tf_op jit(solution)/shard_map/adjoint_steps/pallas_call | solution.py:526
  30.8 0.7 %copy.14 = f32[1,7,1,8,1536]{4,3,2,1,0:T(8,128)} copy(f32[1,7,1,8,1536]{4,3,2,1,0:T(8,128)S(1)} %bitcast.9) | data formatting | bytes 688128

commit v6 on v4

--- a/solution.py
+++ b/solution.py
@@ -495,6 +495,15 @@
 
     fill_base(1, base, out)
 
+    def finish(piece):
+        start, stop = PIECES[piece]
+        take_layers(1, piece)
+        for f in range(FIELDS):
+            out[f, :, start:stop] = with_halos(out[f, :, start:stop], 1, f, start, stop)
+
+    take_rows(1)
+    for piece in range(len(PIECES) - 1):
+        finish(piece)
     add_ghost(1, out)
 
     @pl.when(outer)
@@ -503,11 +512,7 @@
             cols = slice(b * WIDE, (b + 1) * WIDE)
             out[FORCED, :, cols] = out[FORCED, :, cols] + forcing[b * ROWS:(b + 1) * ROWS]
 
-    take_rows(1)
-    for piece, (start, stop) in enumerate(PIECES):
-        take_layers(1, piece)
-        for f in range(FIELDS):
-            out[f, :, start:stop] = with_halos(out[f, :, start:stop], 1, f, start, stop)
+    finish(len(PIECES) - 1)
 
     @pl.when(z == LAYERS - 2)
     def _():

time: 31.5 us -> 31.5 us (level)
  no operation moved by 1% of the time
where the time goes in v6:
time: 31.5 us; the launch traced here: 31.3 us
  Pallas kernels  30.6 us (97%)
  local copies, waits for them, and re-layouts  0.73 us (2%)
    pallas_call x1, Pallas kernels, steps(): pl.pallas_call(kernel, out_shape=pltpu.VMEM(state, F32), in_specs=[pl.Blo...  30.6 us
    unnamed x1, local copies, waits for them, and re-layouts  0.73 us

profile of v6, /device:TPU:1, one launch (start us, length us, event | category | flops | bytes accessed | tf_op | source)
XLA Modules:
  0.0 31.3 jit_solution(13406689157750620112)
XLA Ops:
  0.0 30.6 %adjoint_steps.1 = f32[7,8,1536]{2,1,0:T(8,128)S(1)} custom-call(f32[7,8,1536]{2,1,0:T(8,128)} %bitcast.10, f32[8,1536]{1,0:T(8,128)} %bitcast.11, f32[7]{0:T(128)} %diffus_hbm.1, f32[7,7]{1,0:T(8,128)} %couple_hbm.1, s32[2,4,256]{2,1,0:T(4,128)} %ghost_row_hbm.1, s32[2,4,256]{2,1,0:T(4,128)} %ghost_col_hbm.1, f32[2,4,256]{2,1,0:T(4,128)} %ghost_wt_hbm.1, ...), custom_call_target="tpu_custom_call" | custom-call | tf_op jit(solution)/shard_map/adjoint_steps/pallas_call | solution.py:555
  30.6 0.7 %copy.14 = f32[1,7,1,8,1536]{4,3,2,1,0:T(8,128)} copy(f32[1,7,1,8,1536]{4,3,2,1,0:T(8,128)S(1)} %bitcast.9) | data formatting | bytes 688128
